TPU v7x, 32 devices: a whole 2x2x4 slice. The times are simulated.
32 devices in a mesh: shot: 2 (over y), row: 4 (over x, core), freq: 4 (over z).
Axes of the slice: x: 2, y: 2, z: 4, core: 2. Of those that a mesh axis runs over, the one named last changes fastest.
Arguments:
- source_field: float32 [2, 8, 1024, 1024], P(None, ('shot', 'freq'), 'row'), parts along dimension 1, may hold values from -6 to 6
- receiver_field: float32 [2, 8, 1024, 1024], P(None, ('shot', 'freq'), 'row'), parts along dimension 1, may hold values from -6 to 6
- slowness: float32 [4, 1024, 1024], P('freq', 'row'), may hold values from 0.22 to 0.67
- owner: int32 [4], replicated, may hold values from 0 to 3, each once
- freq_index: int32 [8], P(('shot', 'freq')), parts along dimension 0, may hold values from 0 to 3, each once
Outputs:
- source_out: float32 [2, 8, 1024, 1024], P(None, ('shot', 'freq'), 'row'), parts along dimension 1
- receiver_out: float32 [2, 8, 1024, 1024], P(None, ('shot', 'freq'), 'row'), parts along dimension 1
- image: float32 [4, 1024, 1024], P('shot', 'row', 'freq'), parts along dimension 0
There are 2 independent parts, one for each index of `shot`. A program takes and returns all parts, laid end to end along the dimension named above; an argument that names none is the same for every part. Nothing has to cross between parts.
All inputs are finite; a program needn't handle non-finite values.
Results may differ from a plain program's by a relative error of at most 0.00022.
Values sent between devices are 32-bit elements; how exact they have to be, the bound alone decides.
A program may use at most 128 MiB of HBM per device.

v0:
```python
import math

import jax
import jax.numpy as jnp
from jax import lax
from jax.sharding import PartitionSpec as P

NZ = 2


dz_km = 0.01
dx_km = 0.0125
ref_slow = 0.5
base_hertz = 3.0
step_hertz = 4.0
taper = 0.5


def spread(value, axis, source):
    kept = jnp.where(lax.axis_index(axis) == source, value, 0).astype(value.dtype)
    return lax.psum(kept, axis)


def split_length(length):
    return length // 128


def angle_table(count_a, count_b, modulus, sign):
    left = jnp.arange(count_a, dtype=jnp.int32)[:, None]
    right = jnp.arange(count_b, dtype=jnp.int32)[None, :]
    turns = (left * right % modulus).astype(jnp.float32) * (2.0 * math.pi / modulus)
    return (jnp.cos(turns), sign * jnp.sin(turns))


def contract(form, left, right):
    return jnp.einsum(form, left, right, precision=lax.Precision.HIGHEST)


def transform_pair(real_part, imag_part, sign, last):
    length = real_part.shape[2] if last else real_part.shape[1]
    first = split_length(length)
    second = length // first
    cos_a, sin_a = angle_table(first, first, first, sign)
    cos_b, sin_b = angle_table(second, second, second, sign)
    twist_c, twist_s = angle_table(first, second, length, sign)
    if last:
        shape = (real_part.shape[0], real_part.shape[1], first, second)
        form_one = "fajb,jk->fakb"
        form_two = "fakb,bm->famk"
    else:
        shape = (real_part.shape[0], first, second, real_part.shape[2])
        form_one = "fjbq,jk->fkbq"
        form_two = "fkbq,bm->fmkq"
        twist_c = twist_c[:, :, None]
        twist_s = twist_s[:, :, None]
    x_re = real_part.reshape(shape)
    x_im = imag_part.reshape(shape)
    y_re = contract(form_one, x_re, cos_a) - contract(form_one, x_im, sin_a)
    y_im = contract(form_one, x_im, cos_a) + contract(form_one, x_re, sin_a)
    z_re = y_re * twist_c - y_im * twist_s
    z_im = y_im * twist_c + y_re * twist_s
    out_re = contract(form_two, z_re, cos_b) - contract(form_two, z_im, sin_b)
    out_im = contract(form_two, z_im, cos_b) + contract(form_two, z_re, sin_b)
    return (out_re.reshape(real_part.shape), out_im.reshape(real_part.shape))


def transform(block, sign, last):
    count = block.shape[0]
    freqs = block.shape[2]
    plane = block.shape[3:]
    real_part = block[:, 0].reshape((count * freqs,) + plane)
    imag_part = block[:, 1].reshape((count * freqs,) + plane)
    out_re, out_im = transform_pair(real_part, imag_part, sign, last)
    shape = (count, freqs) + plane
    return jnp.stack([out_re.reshape(shape), out_im.reshape(shape)], axis=1)


def wavenumbers(length, start, count):
    index = start + jnp.arange(count, dtype=jnp.int32)
    signed = jnp.where(index * 2 < length, index, index - length)
    return signed.astype(jnp.float32) * (2.0 * math.pi / (length * dx_km))


def rotate(block, cos_v, sin_v):
    real_part = block[:, 0]
    imag_part = block[:, 1]
    return jnp.stack(
        [real_part * cos_v - imag_part * sin_v, imag_part * cos_v + real_part * sin_v], axis=1
    )


def shift_phase(block, omega, kx_part, ky_part, total):
    square = kx_part[:, None] ** 2 + ky_part[None, :] ** 2
    kmax = math.pi / dx_km
    damp = jnp.exp(-taper * square / (kmax * kmax)) / total
    ws0 = omega[:, None, None] * ref_slow
    vertical = ws0 - 0.5 * square[None] / ws0
    cos_v = jnp.cos(dz_km * vertical) * damp
    sin_v = jnp.sin(dz_km * vertical) * damp
    return rotate(block, cos_v, sin_v)


def correct(block, slab, omega):
    theta = omega[:, None, None] * (slab[None] - ref_slow) * dz_km
    return rotate(block, jnp.cos(theta), jnp.sin(theta))


def image_term(block):
    return jnp.sum(block[0, 0] * block[1, 0] - block[0, 1] * block[1, 1], axis=0)


def body(source_field, receiver_field, slowness, owner, freq_index):
    rows = source_field.shape[2]
    width = source_field.shape[3]
    row_count = lax.axis_size("row")
    height = rows * row_count
    cols = width // row_count
    place = lax.axis_index("row")
    omega = 2.0 * math.pi * (base_hertz + step_hertz * freq_index.astype(jnp.float32))
    mirrored = jnp.stack([receiver_field[0], -receiver_field[1]])
    fields = jnp.stack([source_field, mirrored])
    kx_all = wavenumbers(height, 0, height)
    ky_own = wavenumbers(width, place * cols, cols)
    total = float(height * width)
    slab_dev = slowness.shape[0]
    images = []
    for depth in range(NZ):
        chosen = owner[depth]
        held = spread(slowness, "freq", chosen // slab_dev)
        slab = lax.dynamic_index_in_dim(held, chosen % slab_dev, 0, keepdims=False)
        fields = transform(fields, -1.0, True)
        fields = lax.all_to_all(fields, "row", split_axis=4, concat_axis=3, tiled=True)
        items = fields
        items = transform(items, -1.0, False)
        items = shift_phase(items, omega, kx_all, ky_own, total)
        fields = transform(items, 1.0, False)
        fields = lax.all_to_all(fields, "row", split_axis=3, concat_axis=4, tiled=True)
        fields = transform(fields, 1.0, True)
        fields = correct(fields, slab, omega)
        images.append(image_term(fields))
    parts = [lax.psum_scatter(term, "freq", scatter_dimension=1, tiled=True) for term in images]
    image = jnp.stack(parts)
    source_out = fields[0]
    receiver_out = jnp.stack([fields[1, 0], -fields[1, 1]])
    return (source_out, receiver_out, image)


def solution(mesh):
    in_specs = (
        P(None, ("shot", "freq"), "row", None),
        P(None, ("shot", "freq"), "row", None),
        P("freq", "row", None),
        P(),
        P(("shot", "freq")),
    )
    out_specs = (
        P(None, ("shot", "freq"), "row", None),
        P(None, ("shot", "freq"), "row", None),
        P("shot", "row", "freq"),
    )
    return jax.shard_map(body, mesh=mesh, in_specs=in_specs, out_specs=out_specs, check_vma=False)
```

profile of v0, /device:TPU:2, one launch (start us, length us, event | category | flops | bytes accessed | tf_op | source)
XLA Modules:
  0.0 594.7 jit_solution(643073891319918496)
XLA Ops:
  32.7 5.4 copy.346
  38.1 4.8 all-to-all-start
  44.0 4.0 fusion.186
  48.0 40.6 %all-to-all-done = f32[2,2,1,256,1024]{3,0,2,1,4:T(2,128)} async-done(((f32[2,2,1,256,1024]{3,0,2,1,4:T(2,128)}), f32[2,2,1,256,1024]{3,0,2,1,4:T(2,128)}, u32[]{:S(2)}, u32[]{:S(2)}) %all-to-all-start) | async-done | bytes 4194336 | tf_op jit(solution)/shard_map/all_to_all | solution.py:132
  88.6 5.0 copy.347
  93.6 5.4 copy.348
  110.3 3.8 subtract_bitcast_fusion.13
  136.7 3.9 subtract_bitcast_fusion.11
  154.0 5.2 copy.372
  159.2 7.2 %all-to-all-start.1 = ((f32[2,2,1,1024,256]{4,0,2,1,3:T(2,128)}), f32[2,2,1,1024,256]{4,0,2,1,3:T(2,128)}, u32[]{:S(2)}, u32[]{:S(2)}) async-start(f32[2,2,1,1024,256]{4,0,2,1,3:T(2,128)} %copy.372), calls=%async_computation.1 | async-start | bytes 8388608 | tf_op jit(solution)/shard_map/all_to_all | solution.py:137
  169.9 89.5 %all-reduce.3.cloned.1.call-done = (f32[1,256,1024]{2,1,0:T(8,128)}, f32[1,256,1024]{2,1,0:T(8,128)}) async-done(((f32[1,256,1024]{2,1,0:T(8,128)}, f32[1,256,1024]{2,1,0:T(8,128)}), (f32[1,256,1024]{2,1,0:T(8,128)}, f32[1,256,1024]{2,1,0:T(8,128)})) %all-reduce.3.cloned.1.call-update) | async-done | bytes 2097168 | tf_op jit(solution)/shard_map/psum | solution.py:21
  259.5 4.7 fusion.192
  267.1 5.0 copy.373
  272.1 5.3 copy.374
  277.4 4.6 fusion.663
  313.9 4.8 fusion.314
  321.8 3.6 fusion.316
  342.1 3.2 copy.395
  345.3 49.6 %all_to_all.72 = f32[2,2,1,256,1024]{3,0,2,1,4:T(2,128)S(1)} all-to-all(f32[2,2,1,256,1024]{3,0,2,1,4:T(2,128)S(1)} %copy.395), channel_id=1, replica_groups=mesh['shot'=2,'row'=4,'freq'=4] {'row'}, dimensions={4} | all-to-all | bytes 8388608 | tf_op jit(solution)/shard_map/all_to_all | solution.py:132
  397.7 5.7 copy.397
  414.6 3.6 subtract_bitcast_fusion.5
  440.8 4.0 subtract_bitcast_fusion.3
  458.2 5.2 copy.418
  463.5 6.5 %all-to-all-start.3 = ((f32[2,2,1,1024,256]{4,0,2,1,3:T(2,128)}), f32[2,2,1,1024,256]{4,0,2,1,3:T(2,128)}, u32[]{:S(2)}, u32[]{:S(2)}) async-start(f32[2,2,1,1024,256]{4,0,2,1,3:T(2,128)} %copy.418), calls=%async_computation.3 | async-start | bytes 8388608 | tf_op jit(solution)/shard_map/all_to_all | solution.py:137
  473.9 5.7 cosine_bitcast_fusion
  483.7 4.7 fusion.10
  489.7 26.9 %all-to-all-done.3 = f32[2,2,1,1024,256]{4,0,2,1,3:T(2,128)} async-done(((f32[2,2,1,1024,256]{4,0,2,1,3:T(2,128)}), f32[2,2,1,1024,256]{4,0,2,1,3:T(2,128)}, u32[]{:S(2)}, u32[]{:S(2)}) %all-to-all-start.3) | async-done | bytes 4194336 | tf_op jit(solution)/shard_map/all_to_all | solution.py:137
  516.6 5.0 copy.419
  521.6 5.3 copy.420
  526.8 4.6 fusion.661
  565.4 4.3 fusion.14
  571.6 14.3 %reduce-scatter.5.cloned.1.call-done = f32[256,256]{0,1:T(8,128)} async-done(((f32[256,1024]{0,1:T(8,128)}), f32[256,256]{0,1:T(8,128)}) %reduce-scatter.5.cloned.1.call-update) | async-done | bytes 262160 | tf_op jit(solution)/shard_map/reduce_scatter | solution.py:141
  (169 shorter events, 225.9 us)
Async XLA Ops:
  8.9 1.6 copy-start.19
  38.1 50.5 %all-to-all-start = ((f32[2,2,1,256,1024]{3,0,2,1,4:T(2,128)}), f32[2,2,1,256,1024]{3,0,2,1,4:T(2,128)}, u32[]{:S(2)}, u32[]{:S(2)}) async-start(f32[2,2,1,256,1024]{3,0,2,1,4:T(2,128)} %copy.346), calls=%async_computation | async-start | bytes 8388608 | tf_op jit(solution)/shard_map/all_to_all | solution.py:132
  48.0 79.1 %copy-start.8 = (f32[8,128,256]{2,1,0:T(8,128)}, f32[8,128,256]{2,1,0:T(8,128)S(1)}, u32[]{:S(2)}) copy-start(f32[8,128,256]{2,1,0:T(8,128)S(1)} %get-tuple-element.67) | copy-start | bytes 3145732
  159.2 7.2 %copy-start.21 = (s32[4]{0:T(128)S(1)}, s32[4]{0:T(128)}, u32[]{:S(2)}) copy-start(s32[4]{0:T(128)} %param.8) | copy-start | bytes 52
  159.2 9.1 %copy-start.20 = (f32[1,256,1024]{2,1,0:T(8,128)S(1)}, f32[1,256,1024]{2,1,0:T(8,128)}, u32[]{:S(2)}) copy-start(f32[1,256,1024]{2,1,0:T(8,128)} %param.7) | copy-start | bytes 3145732
  159.2 107.9 %all-to-all-start.1 = ((f32[2,2,1,1024,256]{4,0,2,1,3:T(2,128)}), f32[2,2,1,1024,256]{4,0,2,1,3:T(2,128)}, u32[]{:S(2)}, u32[]{:S(2)}) async-start(f32[2,2,1,1024,256]{4,0,2,1,3:T(2,128)} %copy.372), calls=%async_computation.1 | async-start | bytes 8388608 | tf_op jit(solution)/shard_map/all_to_all | solution.py:137
  166.4 93.0 %all-reduce.3.cloned.1.call-start = ((), (), s32[]{:S(2)}) async-start(), calls=%async_computation.8 | async-start | bytes 4194304 | tf_op jit(solution)/shard_map/psum | solution.py:21
  264.2 2.9 copy-start.11
  264.2 2.9 copy-start.13
  284.1 3.2 copy-start.6
  289.6 1.9 copy-start.14
  291.5 2.0 copy-start.7
  305.6 1.3 copy-start.1
  306.9 1.2 copy-start.17
  306.9 1.5 copy-start.18
  321.8 3.6 copy-start.2
  321.8 3.6 copy-start.15
  325.4 2.0 copy-start.5
  430.1 1.2 copy-start.9
  463.5 53.1 %all-to-all-start.3 = ((f32[2,2,1,1024,256]{4,0,2,1,3:T(2,128)}), f32[2,2,1,1024,256]{4,0,2,1,3:T(2,128)}, u32[]{:S(2)}, u32[]{:S(2)}) async-start(f32[2,2,1,1024,256]{4,0,2,1,3:T(2,128)} %copy.418), calls=%async_computation.3 | async-start | bytes 8388608 | tf_op jit(solution)/shard_map/all_to_all | solution.py:137
  470.0 2.7 copy-start.12
  470.0 101.7 %reduce-scatter.3.cloned.1.call-start = ((), (), s32[]{:S(2)}) async-start(), calls=%async_computation.6 | async-start | bytes 1310720 | tf_op jit(solution)/shard_map/reduce_scatter | solution.py:141
  489.6 96.3 %reduce-scatter.5.cloned.1.call-start = ((), (), s32[]{:S(2)}) async-start(), calls=%async_computation.7 | async-start | bytes 1310720 | tf_op jit(solution)/shard_map/reduce_scatter | solution.py:141
  533.5 3.2 copy-start.3
  539.2 1.9 copy-start.16
  541.1 2.0 copy-start.4
  552.6 2.3 copy-start.10
  554.9 2.5 copy-start
Sparse Core Ops, SparseCore 0:
  170.2 89.1 all-reduce.2
  489.8 26.1 reduce-scatter.2
  559.6 26.2 reduce-scatter.4
where the time goes:
time: 606 us; the launch traced here: 595 us
  waiting for transfers between devices  171 us (28%)
  matrix products  170 us (28%)
  local copies, waits for them, and re-layouts  125 us (21%)
  blocking collectives  49.6 us (8%)
  other arithmetic  42.9 us (7%)
  starting transfers between devices  18.6 us (3%)
  between operations  17.3 us (3%)
    dot_general x64, matrix products, contract(): return jnp.einsum(form, left, right, precision=lax.Precision.HIGHEST)  170 us
    psum x1, waiting for transfers between devices, spread(): return lax.psum(kept, axis)  89.5 us
    all_to_all x1, blocking collectives, body(): lax.all_to_all(fields, 'row', split_axis=4, concat_axis=3, tiled=True)  49.6 us
    all_to_all x1, waiting for transfers between devices, body(): lax.all_to_all(fields, 'row', split_axis=4, concat_axis=3, tiled=True)  40.6 us
    all_to_all x2, waiting for transfers between devices, body(): lax.all_to_all(fields, 'row', split_axis=3, concat_axis=4, tiled=True)  26.9 us
    all_to_all x4, local copies, waits for them, and re-layouts, body(): lax.all_to_all(fields, 'row', split_axis=3, concat_axis=4, tiled=True)  20.5 us
    another operation x4, local copies, waits for them, and re-layouts, transform(): return jnp.stack([out_re.reshape(shape), out_im.reshape(shape)], axis=1)  19.1 us
    all_to_all x4, local copies, waits for them, and re-layouts, body(): lax.all_to_all(fields, 'row', split_axis=4, concat_axis=3, tiled=True)  18.9 us
  transfers between devices with their start and end apart: 6, of which 4 were waited for; matrix products, arithmetic and copies ran while one was open for 15% of the time, Pallas kernels for 0%

commit v1 on v0

v1 whole, which is shorter than its diff:
```python
import math

import jax
import jax.numpy as jnp
from jax import lax
from jax.experimental import pallas as pl
from jax.experimental.pallas import tpu as pltpu
from jax.sharding import PartitionSpec as P

dz_km = 0.01
dx_km = 0.0125
base_hertz = 3.0
step_hertz = 4.0
taper = 0.5
vmem_bytes = 56 * 1024 * 1024


def split_high_low(value):
    high = lax.reduce_precision(value, 8, 7)
    return high.astype(jnp.bfloat16), (value - high).astype(jnp.bfloat16)


def toeplitz_blocks(length, omega):
    quarter = length // 4
    place = jnp.arange(quarter, dtype=jnp.int32)
    kept = 4 * place[None, :] + jnp.arange(4, dtype=jnp.int32)[:, None]
    signed = jnp.where(kept * 2 < length, kept, kept - length)
    square = (signed.astype(jnp.float32) * (2.0 * math.pi / (length * dx_km))) ** 2
    kmax = math.pi / dx_km
    damp = jnp.exp(-taper * square / (kmax * kmax)) / float(length)
    phase = (-dz_km / omega) * square
    amp_r = (damp * jnp.cos(phase))[:, None, :]
    amp_i = (damp * jnp.sin(phase))[:, None, :]
    turns = (kept[:, None, :] * place[None, :, None] % length).astype(jnp.float32)
    turns = turns * (2.0 * math.pi / length)
    cos_v = jnp.cos(turns)
    sin_v = jnp.sin(turns)
    left = jnp.concatenate([cos_v * amp_r - sin_v * amp_i, sin_v * amp_r + cos_v * amp_i], axis=2)
    right = jnp.concatenate(
        [jnp.concatenate([cos_v, sin_v], axis=2), jnp.concatenate([-sin_v, cos_v], axis=2)], axis=1
    )
    both = jnp.einsum("kbm,kcm->kbc", left, right, precision=lax.Precision.HIGHEST)
    return both[:, :, :quarter], both[:, :, quarter:]


def pack(real, imag, sign):
    top = jnp.concatenate([real, -sign * imag], axis=2)
    low = jnp.concatenate([sign * imag, real], axis=2)
    return split_high_low(jnp.concatenate([top, low], axis=1))


def column_matrix(real, imag):
    return pack(real, imag, 1.0)


def row_matrix(real, imag):
    turned_r = jnp.stack([real[0], real[3], real[2], real[1]])
    turned_i = jnp.stack([imag[0], imag[3], imag[2], imag[1]])
    return pack(turned_r, turned_i, -1.0)


def butterfly(re, im, sign):
    sum_r, dif_r = re[0] + re[2], re[0] - re[2]
    sum_i, dif_i = im[0] + im[2], im[0] - im[2]
    odd_r, gap_r = re[1] + re[3], re[1] - re[3]
    odd_i, gap_i = im[1] + im[3], im[1] - im[3]
    if sign < 0:
        gap_r, gap_i = -gap_r, -gap_i
    out_r = [sum_r + odd_r, dif_r - gap_i, sum_r - odd_r, dif_r + gap_i]
    out_i = [sum_i + odd_i, dif_i + gap_r, sum_i - odd_i, dif_i - gap_r]
    return out_r, out_i


def halves(value):
    high = value.astype(jnp.bfloat16)
    return high, (value - high.astype(jnp.float32)).astype(jnp.bfloat16)


def dot(left, right):
    return jnp.dot(left, right, preferred_element_type=jnp.float32)


def filter_rows(re, im, high_ref, low_ref):
    quarter = re[0].shape[1]
    re, im = butterfly(re, im, -1)
    out_r, out_i = [], []
    for k in range(4):
        high, low = halves(jnp.concatenate([re[k], im[k]], axis=1))
        out = dot(high, high_ref[k]) + (dot(low, high_ref[k]) + dot(high, low_ref[k]))
        out_r.append(out[:, :quarter])
        out_i.append(out[:, quarter:])
    return butterfly(out_r, out_i, 1)


def filter_cols(re, im, high_ref, low_ref):
    quarter = re[0].shape[0]
    re, im = butterfly(re, im, -1)
    out_r, out_i = [], []
    for k in range(4):
        high, low = halves(jnp.concatenate([re[k], im[k]], axis=0))
        out = dot(high_ref[k], high) + (dot(high_ref[k], low) + dot(low_ref[k], high))
        out_r.append(out[:quarter])
        out_i.append(out[quarter:])
    return butterfly(out_r, out_i, 1)


def first_kernel(source_ref, receiver_ref, high_ref, low_ref, out_ref):
    rows = source_ref.shape[2]
    quarter = source_ref.shape[3] // 4
    re, im = [], []
    for j in range(4):
        span = pl.ds(j * quarter, quarter)
        re.append(jnp.concatenate([source_ref[0, 0, :, span], receiver_ref[0, 0, :, span]], axis=0))
        im.append(jnp.concatenate([source_ref[1, 0, :, span], -receiver_ref[1, 0, :, span]], axis=0))
    re, im = filter_rows(re, im, high_ref, low_ref)
    for j in range(4):
        out_ref[j, 0, 0] = re[j][:rows]
        out_ref[j, 0, 1] = im[j][:rows]
        out_ref[j, 1, 0] = re[j][rows:]
        out_ref[j, 1, 1] = im[j][rows:]


def middle_kernel(omega_ref, field_ref, slab_ref, high_ref, low_ref, out_ref, term_ref):
    cols = field_ref.shape[4]
    re = [jnp.concatenate([field_ref[j, 0, 0], field_ref[j, 1, 0]], axis=1) for j in range(4)]
    im = [jnp.concatenate([field_ref[j, 0, 1], field_ref[j, 1, 1]], axis=1) for j in range(4)]
    re, im = filter_cols(re, im, high_ref, low_ref)
    for j in range(4):
        theta = slab_ref[j] * (omega_ref[0] * dz_km)
        cos_v, sin_v = jnp.cos(theta), jnp.sin(theta)
        cos_v = jnp.concatenate([cos_v, cos_v], axis=1)
        sin_v = jnp.concatenate([sin_v, sin_v], axis=1)
        re[j], im[j] = re[j] * cos_v - im[j] * sin_v, im[j] * cos_v + re[j] * sin_v
        term_ref[j] = re[j][:, :cols] * re[j][:, cols:] - im[j][:, :cols] * im[j][:, cols:]
    re, im = filter_cols(re, im, high_ref, low_ref)
    for j in range(4):
        out_ref[j, 0, 0] = re[j][:, :cols]
        out_ref[j, 0, 1] = im[j][:, :cols]
        out_ref[j, 1, 0] = re[j][:, cols:]
        out_ref[j, 1, 1] = im[j][:, cols:]


def last_kernel(omega_ref, field_ref, slab_ref, high_ref, low_ref, source_ref, receiver_ref, term_ref):
    rows, quarter = field_ref.shape[3:]
    re = [jnp.concatenate([field_ref[j, 0, 0], field_ref[j, 1, 0]], axis=0) for j in range(4)]
    im = [jnp.concatenate([field_ref[j, 0, 1], field_ref[j, 1, 1]], axis=0) for j in range(4)]
    re, im = filter_rows(re, im, high_ref, low_ref)
    for j in range(4):
        span = pl.ds(j * quarter, quarter)
        theta = slab_ref[:, span] * (omega_ref[0] * dz_km)
        cos_v, sin_v = jnp.cos(theta), jnp.sin(theta)
        cos_v = jnp.concatenate([cos_v, cos_v], axis=0)
        sin_v = jnp.concatenate([sin_v, sin_v], axis=0)
        out_r, out_i = re[j] * cos_v - im[j] * sin_v, im[j] * cos_v + re[j] * sin_v
        term_ref[:, span] = out_r[:rows] * out_r[rows:] - out_i[:rows] * out_i[rows:]
        source_ref[0, 0, :, span] = out_r[:rows]
        source_ref[1, 0, :, span] = out_i[:rows]
        receiver_ref[0, 0, :, span] = out_r[rows:]
        receiver_ref[1, 0, :, span] = -out_i[rows:]


def params():
    return pltpu.CompilerParams(vmem_limit_bytes=vmem_bytes, dimension_semantics=("arbitrary",))


def whole(shape):
    return pl.BlockSpec(shape, lambda i: (0,) * len(shape))


scalar = pl.BlockSpec(memory_space=pltpu.SMEM)


def body(source_field, receiver_field, slowness, owner, freq_index):
    rows, width = source_field.shape[2:]
    row_count = lax.axis_size("row")
    freq_count = lax.axis_size("freq")
    height = rows * row_count
    cols = width // row_count
    quart_w = width // 4
    quart_h = height // 4
    omega = 2.0 * math.pi * (base_hertz + step_hertz * freq_index.astype(jnp.float32))
    slabs = lax.all_gather(slowness, "freq", axis=0, tiled=True)
    slab_first = lax.dynamic_index_in_dim(slabs, owner[0], 0, keepdims=False)
    slab_last = lax.dynamic_index_in_dim(slabs, owner[1], 0, keepdims=False)
    block_w = toeplitz_blocks(width, omega[0])
    block_h = block_w if height == width else toeplitz_blocks(height, omega[0])
    row_high, row_low = row_matrix(*block_w)
    col_high, col_low = column_matrix(*block_h)
    mat_w = whole((4, 2 * quart_w, 2 * quart_w))
    mat_h = whole((4, 2 * quart_h, 2 * quart_h))

    step = min(rows, 64)
    row_block = pl.BlockSpec((2, 1, step, width), lambda i: (0, 0, i, 0))
    quarter_block = pl.BlockSpec((4, 2, 2, step, quart_w), lambda i: (0, 0, 0, i, 0))
    quarter_shape = jax.ShapeDtypeStruct((4, 2, 2, rows, quart_w), jnp.float32)
    fields = pl.pallas_call(
        first_kernel,
        grid=(rows // step,),
        in_specs=[row_block, row_block, mat_w, mat_w],
        out_specs=quarter_block,
        out_shape=quarter_shape,
        compiler_params=params(),
    )(source_field, receiver_field, row_high, row_low)

    if row_count != 4:
        fields = fields.reshape(4, 2, 2, rows, row_count // 4, cols)
        fields = jnp.moveaxis(fields, 4, 1).reshape(row_count, 2, 2, rows, cols)
    fields = lax.all_to_all(fields, "row", split_axis=0, concat_axis=0, tiled=True)
    if row_count != 4:
        fields = fields.reshape(4, row_count // 4, 2, 2, rows, cols)
        fields = jnp.moveaxis(fields, 1, 3).reshape(4, 2, 2, quart_h, cols)
    slab_first = jnp.moveaxis(slab_first.reshape(rows, row_count, cols), 1, 0)
    slab_first = lax.all_to_all(slab_first, "row", split_axis=0, concat_axis=0, tiled=True)
    slab_first = slab_first.reshape(4, quart_h, cols)

    wide = min(cols, 128)
    col_block = pl.BlockSpec((4, 2, 2, quart_h, wide), lambda i: (0, 0, 0, 0, i))
    term_block = pl.BlockSpec((4, quart_h, wide), lambda i: (0, 0, i))
    fields, term = pl.pallas_call(
        middle_kernel,
        grid=(cols // wide,),
        in_specs=[scalar, col_block, term_block, mat_h, mat_h],
        out_specs=[col_block, term_block],
        out_shape=[
            jax.ShapeDtypeStruct((4, 2, 2, quart_h, cols), jnp.float32),
            jax.ShapeDtypeStruct((4, quart_h, cols), jnp.float32),
        ],
        compiler_params=params(),
    )(omega, fields, slab_first, col_high, col_low)

    if row_count != 4:
        fields = fields.reshape(4, 2, 2, row_count // 4, rows, cols)
        fields = jnp.moveaxis(fields, 3, 1).reshape(row_count, 2, 2, rows, cols)
    fields = lax.all_to_all(fields, "row", split_axis=0, concat_axis=0, tiled=True)
    if row_count != 4:
        fields = fields.reshape(4, row_count // 4, 2, 2, rows, cols)
        fields = jnp.moveaxis(fields, 1, 4).reshape(4, 2, 2, rows, quart_w)
    term = term.reshape(height, cols)
    if row_count == freq_count:
        part = lax.psum_scatter(term, "freq", scatter_dimension=0, tiled=True)
        pairs = [
            (r * freq_count + f, f * freq_count + r)
            for r in range(row_count)
            for f in range(freq_count)
        ]
        image_first = lax.ppermute(part, ("row", "freq"), pairs)
    else:
        term = lax.all_to_all(term, "row", split_axis=0, concat_axis=1, tiled=True)
        image_first = lax.psum_scatter(term, "freq", scatter_dimension=1, tiled=True)

    line_block = pl.BlockSpec((step, width), lambda i: (i, 0))
    field_shape = jax.ShapeDtypeStruct(source_field.shape, jnp.float32)
    source_out, receiver_out, term = pl.pallas_call(
        last_kernel,
        grid=(rows // step,),
        in_specs=[scalar, quarter_block, line_block, mat_w, mat_w],
        out_specs=[row_block, row_block, line_block],
        out_shape=[field_shape, field_shape, jax.ShapeDtypeStruct((rows, width), jnp.float32)],
        compiler_params=params(),
    )(omega, fields, slab_last, row_high, row_low)
    image_last = lax.psum_scatter(term, "freq", scatter_dimension=1, tiled=True)
    return source_out, receiver_out, jnp.stack([image_first, image_last])


def solution(mesh):
    in_specs = (
        P(None, ("shot", "freq"), "row", None),
        P(None, ("shot", "freq"), "row", None),
        P("freq", "row", None),
        P(),
        P(("shot", "freq")),
    )
    out_specs = (
        P(None, ("shot", "freq"), "row", None),
        P(None, ("shot", "freq"), "row", None),
        P("shot", "row", "freq"),
    )
    return jax.shard_map(body, mesh=mesh, in_specs=in_specs, out_specs=out_specs, check_vma=False)
```

time: 606 us -> 241 us (0.40); the launches traced: 595 us -> 238 us
  matrix products: 170 us -> 3.69 us
  local copies, waits for them, and re-layouts: 125 us -> 8.33 us
  blocking collectives: 49.6 us -> 0 us
  Pallas kernels: 0 us -> 36.6 us
  waiting for transfers between devices: 171 us -> 137 us
  other arithmetic: 42.9 us -> 15 us
    dot_general x64 -> x1, matrix products: 170 us -> 3.69 us  [toeplitz_blocks(): jnp.einsum('kbm,kcm->kbc', left, right, precision=lax.Precision.HIGHEST)]
    psum x1 -> x0, waiting for transfers between devices: 89.5 us -> none  [spread(): return lax.psum(kept, axis)]
    all_gather x0 -> x1, waiting for transfers between devices: none -> 50.4 us  [body(): slabs = lax.all_gather(slowness, 'freq', axis=0, tiled=True)]
    all_to_all x1 -> x0, blocking collectives: 49.6 us -> none  [body(): lax.all_to_all(fields, 'row', split_axis=4, concat_axis=3, tiled=True)]
    all_to_all x8 -> x0, local copies, waits for them, and re-layouts: 39.4 us -> none  [the longest x4 20.5 us: body(): lax.all_to_all(fields, 'row', split_axis=3, concat_axis=4, tiled=True)]
    pallas_call x0 -> x3, Pallas kernels: none -> 36.6 us  [the longest x1 16.3 us: body(): pl.pallas_call(middle_kernel, grid=(cols // wide,), in_specs=[scalar, col...]
    another operation x8 -> x0, local copies, waits for them, and re-layouts: 28.1 us -> none  [the longest x4 19.1 us: transform(): return jnp.stack([out_re.reshape(shape), out_im.reshape(shape)], axis=1)]
    ppermute x0 -> x1, waiting for transfers between devices: none -> 25.8 us  [body(): image_first = lax.ppermute(part, ('row', 'freq'), pairs)]
  transfers between devices with their start and end apart: 6 -> 7, of which waited for: 4 -> 5; matrix products, arithmetic and copies ran while one was open for 15% -> 10% of each run, Pallas kernels for 0% -> 8%
where the time goes in v1:
time: 241 us; the launch traced here: 238 us
  waiting for transfers between devices  137 us (57%)
  Pallas kernels  36.6 us (15%)
  starting transfers between devices  19.7 us (8%)
  between operations  18.4 us (8%)
  other arithmetic  15 us (6%)
  local copies, waits for them, and re-layouts  8.33 us (3%)
  matrix products  3.69 us (2%)
    all_gather x1, waiting for transfers between devices, body(): slabs = lax.all_gather(slowness, 'freq', axis=0, tiled=True)  50.4 us
    all_to_all x2, waiting for transfers between devices, body(): lax.all_to_all(fields, 'row', split_axis=0, concat_axis=0, tiled=True)  45.8 us
    ppermute x1, waiting for transfers between devices, body(): image_first = lax.ppermute(part, ('row', 'freq'), pairs)  25.8 us
    pallas_call x1, Pallas kernels, body(): pl.pallas_call(middle_kernel, grid=(cols // wide,), in_specs=[scalar, col...  16.3 us
    pallas_call x1, Pallas kernels, body(): pl.pallas_call(last_kernel, grid=(rows // step,), in_specs=[scalar, quart...  11.7 us
    all_to_all x2, starting transfers between devices, body(): lax.all_to_all(fields, 'row', split_axis=0, concat_axis=0, tiled=True)  11.6 us
    all_to_all x1, waiting for transfers between devices, body(): lax.all_to_all(slab_first, 'row', split_axis=0, concat_axis=0, tiled=True)  10.2 us
    convert_element_type x3, other arithmetic, split_high_low(): return (high.astype(jnp.bfloat16), (value - high).astype(jnp.bfloat16))  8.48 us
  transfers between devices with their start and end apart: 7, of which 5 were waited for; matrix products, arithmetic and copies ran while one was open for 10% of the time, Pallas kernels for 8%

profile of v1, /device:TPU:2, one launch (start us, length us, event | category | flops | bytes accessed | tf_op | source)
XLA Modules:
  0.0 238.3 jit_solution(12159198404862093079)
XLA Ops:
  7.2 0.0 all-gather.2.cloned.1.call-start
  7.2 0.7 all-gather.2.cloned.1.call-update
  8.6 0.1 cosine_multiply_fusion
  8.7 4.3 %multiply_subtract_fusion = (f32[4,256,256]{2,1,0:T(8,128)S(1)}, f32[4,256,256]{2,1,0:T(8,128)S(1)}, f32[4,256,256]{2,1,0:T(8,128)S(1)}, f32[4,256,256]{2,1,0:T(8,128)S(1)}, f32[4,256,256]{2,1,0:T(8,128)S(1)}) fusion(f32[4,256]{1,0:T(4,128)S(1)} %get-tuple-element.34, f32[4,256]{1,0:T(4,128)S(1)} %get-tuple-element.33, s32[4,256]{1,0:T(4,128)S(1)} %iota_add_fusion), kind=kLoop, calls=%fused_computation.28 | loop fusion | flops 5505024 | bytes 5255168 | tf_op jit(solution)/shard_map/sub | solution.py:38
  13.0 3.7 %fusion.2 = f32[4,256,512]{2,1,0:T(8,128)S(1)} fusion(f32[4,256,256]{2,1,0:T(8,128)S(1)} %get-tuple-element.32, f32[4,256,256]{2,1,0:T(8,128)S(1)} %get-tuple-element.31, f32[4,256,256]{2,1,0:T(8,128)S(1)} %get-tuple-element.30, f32[4,256,256]{2,1,0:T(8,128)S(1)} %get-tuple-element.29, f32[4,256,256]{2,1,0:T(8,128)S(1)} %get-tuple-element.28), kind=kOutput, calls=%fused_computation.6 | convolution fusion | flops 3224895488 | bytes 7340032 | tf_op jit(solution)/shard_map/kbm,kcm->kbc/dot_general | solution.py:42
  16.7 0.2 fusion.26
  16.9 0.1 maximum_multiply_fusion
  17.0 3.0 %reduce-precision_convert_fusion.1.high_ref = bf16[4,512,512]{2,1,0:T(8,128)(2,1)} fusion(f32[1,256,256]{2,1,0:T(8,128)S(1)} %get-tuple-element.24, f32[1,256,256]{2,1,0:T(8,128)S(1)} %get-tuple-element.25, f32[1,256,256]{2,1,0:T(8,128)S(1)} %get-tuple-element.26, f32[1,256,256]{2,1,0:T(8,128)S(1)} %get-tuple-element.27, ...), kind=kLoop, calls=%fused_computation.3 | loop fusion | flops 14680064 | bytes 5242880 | tf_op jit(solution)/shard_map/convert_element_type | solution.py:20
  19.9 3.1 %fusion.low_ref = bf16[4,512,512]{2,1,0:T(8,128)(2,1)} fusion(f32[1,256,256]{2,1,0:T(8,128)S(1)} %get-tuple-element.24, f32[1,256,256]{2,1,0:T(8,128)S(1)} %get-tuple-element.25, f32[1,256,256]{2,1,0:T(8,128)S(1)} %get-tuple-element.26, f32[1,256,256]{2,1,0:T(8,128)S(1)} %get-tuple-element.27, f32[4,256,256]{2,1,0:T(8,128)S(1)} %maximum_multiply_fusion, ...), kind=kLoop, calls=%fused_computation.4 | loop fusion | flops 15728640 | bytes 5242880 | tf_op jit(solution)/shard_map/convert_element_type | solution.py:20
  23.1 8.5 %shard_map.76 = f32[4,2,2,256,256]{4,3,2,1,0:T(8,128)} custom-call(f32[2,1,256,1024]{3,2,1,0:T(8,128)} %source_ref.1, f32[2,1,256,1024]{3,2,1,0:T(8,128)} %receiver_ref.1, bf16[4,512,512]{2,1,0:T(8,128)(2,1)} %reduce-precision_convert_fusion.1.high_ref, bf16[4,512,512]{2,1,0:T(8,128)(2,1)} %fusion.low_ref), custom_call_target="tpu_custom_call" | custom-call | tf_op jit(solution)/shard_map/pallas_call | solution.py:196
  31.6 5.1 %all-to-all-start = ((f32[4,2,2,256,256]{4,3,2,1,0:T(8,128)}), f32[4,2,2,256,256]{4,3,2,1,0:T(8,128)}, u32[]{:S(2)}, u32[]{:S(2)}) async-start(f32[4,2,2,256,256]{4,3,2,1,0:T(8,128)} %shard_map.76), calls=%async_computation | async-start | bytes 8388608 | tf_op jit(solution)/shard_map/all_to_all | solution.py:208
  36.7 0.6 fusion.27
  41.2 50.4 %all-gather.2.cloned.1.call-done = f32[4,256,1024]{2,1,0:T(8,128)} async-done(((f32[1,256,1024]{2,1,0:T(8,128)}), f32[4,256,1024]{2,1,0:T(8,128)}) %all-gather.2.cloned.1.call-update) | async-done | bytes 4194320 | tf_op jit(solution)/shard_map/all_gather | solution.py:182
  91.6 2.7 %dynamic-slice_bitcast_fusion = (f32[256,1024]{1,0:T(8,128)}, f32[1,256,1024]{2,1,0:T(8,128)S(1)}) fusion(f32[4,256,1024]{2,1,0:T(8,128)} %all-gather.2.cloned.1.call-done, s32[]{:T(128)S(6)} %select_n.46, s32[]{:T(128)S(6)} %select_n.45), kind=kLoop, calls=%fused_computation.26 | loop fusion | bytes 4194312 | tf_op jit(solution)/shard_map/jit(dynamic_index_in_dim)/squeeze | solution.py:184
  94.4 1.3 copy.13
  95.7 2.5 %copy.12 = f32[256,4,256]{2,0,1:T(8,128)} copy(f32[256,4,256]{0,2,1:T(8,128)} %bitcast.11) | data formatting | bytes 2097152 | tf_op jit(solution)/shard_map/reshape | solution.py:212
  98.2 4.0 %all-to-all-start.1 = ((f32[4,256,256]{2,1,0:T(8,128)}), f32[4,256,256]{2,1,0:T(8,128)S(1)}, u32[]{:S(2)}, u32[]{:S(2)}) async-start(f32[4,256,256]{2,1,0:T(8,128)} %bitcast.10), calls=%async_computation.1 | async-start | bytes 2097152 | tf_op jit(solution)/shard_map/all_to_all | solution.py:213
  102.2 0.3 broadcast_multiply_fusion
  102.5 2.4 fusion.1
  104.8 10.2 %all-to-all-done.1.slab_ref = f32[4,256,256]{2,1,0:T(8,128)S(1)} async-done(((f32[4,256,256]{2,1,0:T(8,128)}), f32[4,256,256]{2,1,0:T(8,128)S(1)}, u32[]{:S(2)}, u32[]{:S(2)}) %all-to-all-start.1) | async-done | bytes 1048608 | tf_op jit(solution)/shard_map/all_to_all | solution.py:213
  115.0 1.0 copy-done
  116.0 16.3 %shard_map.77 = (f32[4,2,2,256,256]{4,3,2,1,0:T(8,128)}, f32[4,256,256]{2,1,0:T(8,128)}) custom-call(f32[1]{0:T(128)S(6)} %mul.212.omega_ref, f32[4,2,2,256,256]{4,3,2,1,0:T(8,128)} %all-to-all-done.field_ref, f32[4,256,256]{2,1,0:T(8,128)} %copy-done, bf16[4,512,512]{2,1,0:T(8,128)(2,1)} %get-tuple-element.16.high_ref, ...), custom_call_target="tpu_custom_call" | custom-call | tf_op jit(solution)/shard_map/pallas_call | solution.py:219
  132.3 6.5 %all-to-all-start.2 = ((f32[4,2,2,256,256]{4,3,2,1,0:T(8,128)}), f32[4,2,2,256,256]{4,3,2,1,0:T(8,128)}, u32[]{:S(2)}, u32[]{:S(2)}) async-start(f32[4,2,2,256,256]{4,3,2,1,0:T(8,128)} %get-tuple-element.8), calls=%async_computation.2 | async-start | bytes 8388608 | tf_op jit(solution)/shard_map/all_to_all | solution.py:234
  138.8 0.7 reduce-scatter.3.cloned.1.call-update
  139.5 0.0 reduce-scatter.5.cloned.1.call-start
  139.6 45.8 %all-to-all-done.2.field_ref = f32[4,2,2,256,256]{4,3,2,1,0:T(8,128)} async-done(((f32[4,2,2,256,256]{4,3,2,1,0:T(8,128)}), f32[4,2,2,256,256]{4,3,2,1,0:T(8,128)}, u32[]{:S(2)}, u32[]{:S(2)}) %all-to-all-start.2) | async-done | bytes 4194336 | tf_op jit(solution)/shard_map/all_to_all | solution.py:234
  185.4 11.7 %shard_map.78 = (f32[2,1,256,1024]{3,2,1,0:T(8,128)}, f32[2,1,256,1024]{3,2,1,0:T(8,128)}, f32[256,1024]{1,0:T(8,128)}) custom-call(f32[1]{0:T(128)S(6)} %mul.212.omega_ref, f32[4,2,2,256,256]{4,3,2,1,0:T(8,128)} %all-to-all-done.2.field_ref, f32[256,1024]{1,0:T(8,128)} %get-tuple-element.13.slab_ref, ...), custom_call_target="tpu_custom_call" | custom-call | tf_op jit(solution)/shard_map/pallas_call | solution.py:253
  197.2 0.0 reduce-scatter.3.cloned.1.call-done
  197.2 4.0 %collective-permute-start = (f32[256,256]{1,0:T(8,128)}, f32[256,256]{1,0:T(8,128)S(1)}, u32[]{:S(2)}, u32[]{:S(2)}) collective-permute-start(f32[256,256]{1,0:T(8,128)} %reduce-scatter.3.cloned.1.call-done), channel_id=1, source_target_pairs={{0,0},{1,4},{2,8},{3,12},{4,1},{5,5},{6,9},{7,13},{8,2},{9,6},{10,... | collective-permute-start | bytes 786440 | tf_op jit(solution)/shard_map/ppermute | solution.py:246
  201.2 25.8 %collective-permute-done = f32[256,256]{1,0:T(8,128)S(1)} collective-permute-done((f32[256,256]{1,0:T(8,128)}, f32[256,256]{1,0:T(8,128)S(1)}, u32[]{:S(2)}, u32[]{:S(2)}) %collective-permute-start) | collective-permute-done | bytes 262176 | tf_op jit(solution)/shard_map/ppermute | solution.py:246
  227.0 3.0 %reduce-scatter.5.cloned.1.call-done = f32[256,256]{1,0:T(8,128)} async-done(((f32[256,1024]{1,0:T(8,128)}), f32[256,256]{1,0:T(8,128)}) %reduce-scatter.5.cloned.1.call-update) | async-done | bytes 262160 | tf_op jit(solution)/shard_map/reduce_scatter | solution.py:261
  230.0 1.8 pad_maximum_fusion
  (8 shorter events, 0.0 us)
Async XLA Ops:
  7.2 84.5 %all-gather.2.cloned.1.call-start = ((), (), s32[]{:S(2)}) async-start(), calls=%async_computation.5 | async-start | bytes 5242880 | tf_op jit(solution)/shard_map/all_gather | solution.py:182
  31.6 5.2 %copy-start.1 = (s32[4]{0:T(128)S(1)}, s32[4]{0:T(128)}, u32[]{:S(2)}) copy-start(s32[4]{0:T(128)} %param.8) | copy-start | bytes 52
  31.6 66.6 %all-to-all-start = ((f32[4,2,2,256,256]{4,3,2,1,0:T(8,128)}), f32[4,2,2,256,256]{4,3,2,1,0:T(8,128)}, u32[]{:S(2)}, u32[]{:S(2)}) async-start(f32[4,2,2,256,256]{4,3,2,1,0:T(8,128)} %shard_map.76), calls=%async_computation | async-start | bytes 8388608 | tf_op jit(solution)/shard_map/all_to_all | solution.py:208
  98.2 16.8 %all-to-all-start.1 = ((f32[4,256,256]{2,1,0:T(8,128)}), f32[4,256,256]{2,1,0:T(8,128)S(1)}, u32[]{:S(2)}, u32[]{:S(2)}) async-start(f32[4,256,256]{2,1,0:T(8,128)} %bitcast.10), calls=%async_computation.1 | async-start | bytes 2097152 | tf_op jit(solution)/shard_map/all_to_all | solution.py:213
  115.0 1.0 copy-start
  132.3 53.1 %all-to-all-start.2 = ((f32[4,2,2,256,256]{4,3,2,1,0:T(8,128)}), f32[4,2,2,256,256]{4,3,2,1,0:T(8,128)}, u32[]{:S(2)}, u32[]{:S(2)}) async-start(f32[4,2,2,256,256]{4,3,2,1,0:T(8,128)} %get-tuple-element.8), calls=%async_computation.2 | async-start | bytes 8388608 | tf_op jit(solution)/shard_map/all_to_all | solution.py:234
  138.8 58.4 %reduce-scatter.3.cloned.1.call-start = ((), (), s32[]{:S(2)}) async-start(), calls=%async_computation.6 | async-start | bytes 1310720 | tf_op jit(solution)/shard_map/reduce_scatter | solution.py:240
  139.5 90.5 %reduce-scatter.5.cloned.1.call-start = ((), (), s32[]{:S(2)}) async-start(), calls=%async_computation.7 | async-start | bytes 1310720 | tf_op jit(solution)/shard_map/reduce_scatter | solution.py:261
  197.2 29.8 %collective-permute-start = (f32[256,256]{1,0:T(8,128)}, f32[256,256]{1,0:T(8,128)S(1)}, u32[]{:S(2)}, u32[]{:S(2)}) collective-permute-start(f32[256,256]{1,0:T(8,128)} %reduce-scatter.3.cloned.1.call-done), channel_id=1, source_target_pairs={{0,0},{1,4},{2,8},{3,12},{4,1},{5,5},{6,9},{7,13},{8,2},{9,6},{10,... | collective-permute-start | bytes 786440 | tf_op jit(solution)/shard_map/ppermute | solution.py:246
Sparse Core Ops, SparseCore 0:
  9.6 82.0 all-gather.1
  141.9 25.6 reduce-scatter.2
  197.3 32.6 reduce-scatter.4

commit v2 on v1

v2 whole, which is shorter than its diff:
```python
import math
from functools import partial

import jax
import jax.numpy as jnp
from jax import lax
from jax.experimental import pallas as pl
from jax.experimental.pallas import tpu as pltpu
from jax.sharding import PartitionSpec as P

dz_km = 0.01
dx_km = 0.0125
base_hertz = 3.0
step_hertz = 4.0
taper = 0.5
vmem_bytes = 56 * 1024 * 1024


def split_high_low(value):
    high = lax.reduce_precision(value, 8, 7)
    return high.astype(jnp.bfloat16), (value - high).astype(jnp.bfloat16)


def toeplitz_blocks(length, omega):
    quarter = length // 4
    place = jnp.arange(quarter, dtype=jnp.int32)
    kept = 4 * place[None, :] + jnp.arange(4, dtype=jnp.int32)[:, None]
    signed = jnp.where(kept * 2 < length, kept, kept - length)
    square = (signed.astype(jnp.float32) * (2.0 * math.pi / (length * dx_km))) ** 2
    kmax = math.pi / dx_km
    damp = jnp.exp(-taper * square / (kmax * kmax)) / float(length)
    phase = (-dz_km / omega) * square
    amp_r = (damp * jnp.cos(phase))[:, None, :]
    amp_i = (damp * jnp.sin(phase))[:, None, :]
    turns = (kept[:, None, :] * place[None, :, None] % length).astype(jnp.float32)
    turns = turns * (2.0 * math.pi / length)
    cos_v = jnp.cos(turns)
    sin_v = jnp.sin(turns)
    left = jnp.concatenate([cos_v * amp_r - sin_v * amp_i, sin_v * amp_r + cos_v * amp_i], axis=2)
    right = jnp.concatenate(
        [jnp.concatenate([cos_v, sin_v], axis=2), jnp.concatenate([-sin_v, cos_v], axis=2)], axis=1
    )
    both = jnp.einsum("kbm,kcm->kbc", left, right, precision=lax.Precision.HIGHEST)
    return both[:, :, :quarter], both[:, :, quarter:]


def pack(real, imag, sign):
    top = jnp.concatenate([real, -sign * imag], axis=2)
    low = jnp.concatenate([sign * imag, real], axis=2)
    return split_high_low(jnp.concatenate([top, low], axis=1))


def column_matrix(real, imag):
    return pack(real, imag, 1.0)


def row_matrix(real, imag):
    turned_r = jnp.stack([real[0], real[3], real[2], real[1]])
    turned_i = jnp.stack([imag[0], imag[3], imag[2], imag[1]])
    return pack(turned_r, turned_i, -1.0)


def butterfly(re, im, sign):
    sum_r, dif_r = re[0] + re[2], re[0] - re[2]
    sum_i, dif_i = im[0] + im[2], im[0] - im[2]
    odd_r, gap_r = re[1] + re[3], re[1] - re[3]
    odd_i, gap_i = im[1] + im[3], im[1] - im[3]
    if sign < 0:
        gap_r, gap_i = -gap_r, -gap_i
    out_r = [sum_r + odd_r, dif_r - gap_i, sum_r - odd_r, dif_r + gap_i]
    out_i = [sum_i + odd_i, dif_i + gap_r, sum_i - odd_i, dif_i - gap_r]
    return out_r, out_i


def halves(value):
    high = value.astype(jnp.bfloat16)
    return high, (value - high.astype(jnp.float32)).astype(jnp.bfloat16)


def dot(left, right):
    return jnp.dot(left, right, preferred_element_type=jnp.float32)


def filter_rows(re, im, high_ref, low_ref):
    quarter = re[0].shape[1]
    re, im = butterfly(re, im, -1)
    out_r, out_i = [], []
    for k in range(4):
        high, low = halves(jnp.concatenate([re[k], im[k]], axis=1))
        out = dot(high, high_ref[k]) + (dot(low, high_ref[k]) + dot(high, low_ref[k]))
        out_r.append(out[:, :quarter])
        out_i.append(out[:, quarter:])
    return butterfly(out_r, out_i, 1)


def filter_cols(re, im, high_ref, low_ref):
    quarter = re[0].shape[0]
    re, im = butterfly(re, im, -1)
    out_r, out_i = [], []
    for k in range(4):
        high, low = halves(jnp.concatenate([re[k], im[k]], axis=0))
        out = dot(high_ref[k], high) + (dot(high_ref[k], low) + dot(low_ref[k], high))
        out_r.append(out[:quarter])
        out_i.append(out[quarter:])
    return butterfly(out_r, out_i, 1)


def first_kernel(sign, field_ref, high_ref, low_ref, out_ref):
    quarter = field_ref.shape[3] // 4
    re, im = [], []
    for j in range(4):
        span = pl.ds(j * quarter, quarter)
        re.append(field_ref[0, 0, :, span])
        im.append(sign * field_ref[1, 0, :, span])
    re, im = filter_rows(re, im, high_ref, low_ref)
    for j in range(4):
        out_ref[j, 0] = re[j]
        out_ref[j, 1] = im[j]


def middle_step(cos_ref, sin_ref, field_ref, high_ref, low_ref, out_ref, keep):
    re = [field_ref[j, 0] for j in range(4)]
    im = [field_ref[j, 1] for j in range(4)]
    re, im = filter_cols(re, im, high_ref, low_ref)
    for j in range(4):
        cos_v, sin_v = cos_ref[j], sin_ref[j]
        re[j], im[j] = re[j] * cos_v - im[j] * sin_v, im[j] * cos_v + re[j] * sin_v
        keep(j, re[j], im[j])
    re, im = filter_cols(re, im, high_ref, low_ref)
    for j in range(4):
        out_ref[j, 0] = re[j]
        out_ref[j, 1] = im[j]


def middle_source(cos_ref, sin_ref, field_ref, high_ref, low_ref, out_ref, mid_ref):
    def keep(j, re, im):
        mid_ref[j, 0] = re
        mid_ref[j, 1] = im

    middle_step(cos_ref, sin_ref, field_ref, high_ref, low_ref, out_ref, keep)


def middle_receiver(cos_ref, sin_ref, field_ref, high_ref, low_ref, mid_ref, out_ref, term_ref):
    def keep(j, re, im):
        term_ref[j] = mid_ref[j, 0] * re - mid_ref[j, 1] * im

    middle_step(cos_ref, sin_ref, field_ref, high_ref, low_ref, out_ref, keep)


def last_step(cos_ref, sin_ref, field_ref, high_ref, low_ref, keep):
    quarter = field_ref.shape[3]
    re = [field_ref[j, 0] for j in range(4)]
    im = [field_ref[j, 1] for j in range(4)]
    re, im = filter_rows(re, im, high_ref, low_ref)
    for j in range(4):
        span = pl.ds(j * quarter, quarter)
        cos_v, sin_v = cos_ref[:, span], sin_ref[:, span]
        keep(span, re[j] * cos_v - im[j] * sin_v, im[j] * cos_v + re[j] * sin_v)


def last_source(cos_ref, sin_ref, field_ref, high_ref, low_ref, source_ref):
    def keep(span, re, im):
        source_ref[0, 0, :, span] = re
        source_ref[1, 0, :, span] = im

    last_step(cos_ref, sin_ref, field_ref, high_ref, low_ref, keep)


def last_receiver(cos_ref, sin_ref, field_ref, high_ref, low_ref, source_ref, receiver_ref, term_ref):
    def keep(span, re, im):
        term_ref[:, span] = source_ref[0, 0, :, span] * re - source_ref[1, 0, :, span] * im
        receiver_ref[0, 0, :, span] = re
        receiver_ref[1, 0, :, span] = -im

    last_step(cos_ref, sin_ref, field_ref, high_ref, low_ref, keep)


def params():
    return pltpu.CompilerParams(vmem_limit_bytes=vmem_bytes, dimension_semantics=("arbitrary",))


def whole(shape):
    return pl.BlockSpec(shape, lambda i: (0,) * len(shape))


def swap(blocks):
    return lax.all_to_all(blocks, "row", split_axis=0, concat_axis=0, tiled=True)


def body(source_field, receiver_field, slowness, owner, freq_index):
    rows, width = source_field.shape[2:]
    row_count = lax.axis_size("row")
    freq_count = lax.axis_size("freq")
    height = rows * row_count
    cols = width // row_count
    quart_w = width // 4
    quart_h = height // 4
    more = row_count // 4
    omega = 2.0 * math.pi * (base_hertz + step_hertz * freq_index.astype(jnp.float32))

    def turning(slab):
        theta = slab * (omega[0] * dz_km)
        return jnp.cos(theta), jnp.sin(theta)

    def owned(depth):
        return jnp.where(lax.axis_index("freq") == owner[depth], slowness[0], 0.0)

    turned = swap(jnp.moveaxis(owned(0).reshape(rows, row_count, cols), 1, 0))
    source_field, turned = lax.optimization_barrier((source_field, turned))
    piece = lax.psum_scatter(turned, "freq", scatter_dimension=0, tiled=True)
    receiver_field, piece = lax.optimization_barrier((receiver_field, piece))
    slab_first = lax.all_gather(piece, "freq", axis=0, tiled=True)
    slab, slab_first = lax.optimization_barrier((owned(1), slab_first))
    slab_last = lax.psum(slab, "freq")
    turn_first = turning(slab_first.reshape(4, quart_h, cols))
    turn_last = turning(slab_last)

    block_w = toeplitz_blocks(width, omega[0])
    block_h = block_w if height == width else toeplitz_blocks(height, omega[0])
    row_high, row_low = row_matrix(*block_w)
    col_high, col_low = column_matrix(*block_h)
    mat_w = whole((4, 2 * quart_w, 2 * quart_w))
    mat_h = whole((4, 2 * quart_h, 2 * quart_h))

    step = min(rows, 128)
    row_block = pl.BlockSpec((2, 1, step, width), lambda i: (0, 0, i, 0))
    quarter_block = pl.BlockSpec((4, 2, step, quart_w), lambda i: (0, 0, i, 0))
    line_block = pl.BlockSpec((step, width), lambda i: (i, 0))
    col_block = pl.BlockSpec((4, 2, quart_h, cols), lambda i: (0, 0, 0, 0))
    term_block = pl.BlockSpec((4, quart_h, cols), lambda i: (0, 0, 0))
    quarter_shape = jax.ShapeDtypeStruct((4, 2, rows, quart_w), jnp.float32)
    col_shape = jax.ShapeDtypeStruct((4, 2, quart_h, cols), jnp.float32)
    term_shape = jax.ShapeDtypeStruct((4, quart_h, cols), jnp.float32)
    line_shape = jax.ShapeDtypeStruct((rows, width), jnp.float32)
    field_shape = jax.ShapeDtypeStruct(source_field.shape, jnp.float32)

    def first(field, sign):
        return pl.pallas_call(
            partial(first_kernel, sign),
            grid=(rows // step,),
            in_specs=[row_block, mat_w, mat_w],
            out_specs=quarter_block,
            out_shape=quarter_shape,
            compiler_params=params(),
        )(field, row_high, row_low)

    def to_cols(fields):
        if more > 1:
            fields = fields.reshape(4, 2, rows, more, cols)
            fields = jnp.moveaxis(fields, 3, 1).reshape(row_count, 2, rows, cols)
        fields = swap(fields)
        if more > 1:
            fields = fields.reshape(4, more, 2, rows, cols)
            fields = jnp.moveaxis(fields, 1, 2).reshape(4, 2, quart_h, cols)
        return fields

    def to_rows(fields):
        if more > 1:
            fields = fields.reshape(4, 2, more, rows, cols)
            fields = jnp.moveaxis(fields, 2, 1).reshape(row_count, 2, rows, cols)
        fields = swap(fields)
        if more > 1:
            fields = fields.reshape(4, more, 2, rows, cols)
            fields = jnp.moveaxis(fields, 1, 3).reshape(4, 2, rows, quart_w)
        return fields

    source = to_cols(first(source_field, 1.0))
    receiver = to_cols(first(receiver_field, -1.0))
    source, middle = pl.pallas_call(
        middle_source,
        grid=(1,),
        in_specs=[term_block, term_block, col_block, mat_h, mat_h],
        out_specs=[col_block, col_block],
        out_shape=[col_shape, col_shape],
        compiler_params=params(),
    )(*turn_first, source, col_high, col_low)
    source = to_rows(source)
    receiver, term = pl.pallas_call(
        middle_receiver,
        grid=(1,),
        in_specs=[term_block, term_block, col_block, mat_h, mat_h, col_block],
        out_specs=[col_block, term_block],
        out_shape=[col_shape, term_shape],
        compiler_params=params(),
    )(*turn_first, receiver, col_high, col_low, middle)
    receiver = to_rows(receiver)

    term = term.reshape(height, cols)
    if row_count == freq_count:
        part = lax.psum_scatter(term, "freq", scatter_dimension=0, tiled=True)
        pairs = [
            (r * freq_count + f, f * freq_count + r)
            for r in range(row_count)
            for f in range(freq_count)
        ]
        image_first = lax.ppermute(part, ("row", "freq"), pairs)
    else:
        term = lax.all_to_all(term, "row", split_axis=0, concat_axis=1, tiled=True)
        image_first = lax.psum_scatter(term, "freq", scatter_dimension=1, tiled=True)

    source_out = pl.pallas_call(
        last_source,
        grid=(rows // step,),
        in_specs=[line_block, line_block, quarter_block, mat_w, mat_w],
        out_specs=row_block,
        out_shape=field_shape,
        compiler_params=params(),
    )(*turn_last, source, row_high, row_low)
    receiver_out, term = pl.pallas_call(
        last_receiver,
        grid=(rows // step,),
        in_specs=[line_block, line_block, quarter_block, mat_w, mat_w, row_block],
        out_specs=[row_block, line_block],
        out_shape=[field_shape, line_shape],
        compiler_params=params(),
    )(*turn_last, receiver, row_high, row_low, source_out)
    image_last = lax.psum_scatter(term, "freq", scatter_dimension=1, tiled=True)
    return source_out, receiver_out, jnp.stack([image_first, image_last])


def solution(mesh):
    in_specs = (
        P(None, ("shot", "freq"), "row", None),
        P(None, ("shot", "freq"), "row", None),
        P("freq", "row", None),
        P(),
        P(("shot", "freq")),
    )
    out_specs = (
        P(None, ("shot", "freq"), "row", None),
        P(None, ("shot", "freq"), "row", None),
        P("shot", "row", "freq"),
    )
    return jax.shard_map(body, mesh=mesh, in_specs=in_specs, out_specs=out_specs, check_vma=False)
```

time: 241 us -> 241 us (level)
  waiting for transfers between devices: 137 us -> 105 us
  other arithmetic: 15 us -> 31.3 us
  starting transfers between devices: 19.7 us -> 28.2 us
  Pallas kernels: 36.6 us -> 43.7 us
  between operations: 18.4 us -> 15.9 us
    all_gather x1, waiting for transfers between devices: 50.4 us -> 4.93 us  [body(): slab_first = lax.all_gather(piece, 'freq', axis=0, tiled=True)]
    all_to_all x3 -> x5, waiting for transfers between devices: 56 us -> 22.6 us  [swap(): lax.all_to_all(blocks, 'row', split_axis=0, concat_axis=0, tiled=True)]
    psum x0 -> x1, waiting for transfers between devices: none -> 27.7 us  [body(): slab_last = lax.psum(slab, 'freq')]
    reduce_scatter x0 -> x1, waiting for transfers between devices: none -> 11.4 us  [body(): piece = lax.psum_scatter(turned, 'freq', scatter_dimension=0, tiled=True)]
    sin x0 -> x2, other arithmetic: none -> 11.4 us  [turning(): return (jnp.cos(theta), jnp.sin(theta))]
    all_to_all x3 -> x5, starting transfers between devices: 15.6 us -> 25.2 us  [swap(): lax.all_to_all(blocks, 'row', split_axis=0, concat_axis=0, tiled=True)]
    reduce_scatter x1, waiting for transfers between devices: 0.02 us -> 8.43 us  [body(): part = lax.psum_scatter(term, 'freq', scatter_dimension=0, tiled=True)]
    pallas_call x3 -> x6, Pallas kernels: 36.6 us -> 43.7 us  [the longest x2 11.6 us: first(): pl.pallas_call(partial(first_kernel, sign), grid=(rows // step,), in_spec...]
  transfers between devices with their start and end apart: 7 -> 11, of which waited for: 5 -> 10; matrix products, arithmetic and copies ran while one was open for 10% -> 13% of each run, Pallas kernels for 8% -> 18%
where the time goes in v2:
time: 241 us; the launch traced here: 237 us
  waiting for transfers between devices  105 us (44%)
  Pallas kernels  43.7 us (18%)
  other arithmetic  31.3 us (13%)
  starting transfers between devices  28.2 us (12%)
  between operations  15.9 us (7%)
  local copies, waits for them, and re-layouts  9.6 us (4%)
  matrix products  3.71 us (2%)
    psum x1, waiting for transfers between devices, body(): slab_last = lax.psum(slab, 'freq')  27.7 us
    ppermute x1, waiting for transfers between devices, body(): image_first = lax.ppermute(part, ('row', 'freq'), pairs)  27.2 us
    all_to_all x5, starting transfers between devices, swap(): lax.all_to_all(blocks, 'row', split_axis=0, concat_axis=0, tiled=True)  25.2 us
    all_to_all x5, waiting for transfers between devices, swap(): lax.all_to_all(blocks, 'row', split_axis=0, concat_axis=0, tiled=True)  22.6 us
    pallas_call x2, Pallas kernels, first(): pl.pallas_call(partial(first_kernel, sign), grid=(rows // step,), in_spec...  11.6 us
    reduce_scatter x1, waiting for transfers between devices, body(): piece = lax.psum_scatter(turned, 'freq', scatter_dimension=0, tiled=True)  11.4 us
    sin x2, other arithmetic, turning(): return (jnp.cos(theta), jnp.sin(theta))  11.4 us
    pallas_call x1, Pallas kernels, body(): pl.pallas_call(middle_receiver, grid=(1,), in_specs=[term_block, term_blo...  9.83 us
  transfers between devices with their start and end apart: 11, of which 10 were waited for; matrix products, arithmetic and copies ran while one was open for 13% of the time, Pallas kernels for 18%

profile of v2, /device:TPU:2, one launch (start us, length us, event | category | flops | bytes accessed | tf_op | source)
XLA Modules:
  0.0 237.5 jit_solution(11406086166715292006)
XLA Ops:
  9.8 2.5 %broadcast_select_fusion = (f32[1,256,1024]{2,1,0:T(8,128)S(1)}, f32[256,1024]{1,0:T(8,128)}) fusion(f32[1,256,1024]{2,1,0:T(8,128)} %param.7, pred[]{:T(512)S(6)} %eq.9, pred[]{:T(512)S(6)} %eq.8), kind=kLoop, calls=%fused_computation.42 | loop fusion | flops 524288 | bytes 3145730 | tf_op jit(solution)/shard_map/jit(_where)/select_n | solution.py:206
  13.9 3.5 %all-to-all-start = ((f32[4,256,256]{2,1,0:T(8,128)}), f32[4,256,256]{2,1,0:T(8,128)S(1)}, u32[]{:S(2)}, u32[]{:S(2)}) async-start(f32[4,256,256]{2,1,0:T(8,128)} %bitcast.11), calls=%async_computation | async-start | bytes 2097152 | tf_op jit(solution)/shard_map/all_to_all | solution.py:187
  18.3 4.3 %multiply_subtract_fusion = (f32[4,256,256]{2,1,0:T(8,128)S(1)}, f32[4,256,256]{2,1,0:T(8,128)S(1)}, f32[4,256,256]{2,1,0:T(8,128)S(1)}, f32[4,256,256]{2,1,0:T(8,128)S(1)}, f32[4,256,256]{2,1,0:T(8,128)S(1)}) fusion(f32[4,256]{1,0:T(4,128)S(1)} %get-tuple-element.52, f32[4,256]{1,0:T(4,128)S(1)} %get-tuple-element.51, s32[4,256]{1,0:T(4,128)S(1)} %iota_add_fusion), kind=kLoop, calls=%fused_computation.28 | loop fusion | flops 5505024 | bytes 5255168 | tf_op jit(solution)/shard_map/sub | solution.py:39
  22.6 3.7 %fusion.2 = f32[4,256,512]{2,1,0:T(8,128)S(1)} fusion(f32[4,256,256]{2,1,0:T(8,128)S(1)} %get-tuple-element.50, f32[4,256,256]{2,1,0:T(8,128)S(1)} %get-tuple-element.49, f32[4,256,256]{2,1,0:T(8,128)S(1)} %get-tuple-element.48, f32[4,256,256]{2,1,0:T(8,128)S(1)} %get-tuple-element.47, f32[4,256,256]{2,1,0:T(8,128)S(1)} %get-tuple-element.46), kind=kOutput, calls=%fused_computation.6 | convolution fusion | flops 3224895488 | bytes 7340032 | tf_op jit(solution)/shard_map/kbm,kcm->kbc/dot_general | solution.py:43
  28.0 2.1 all-to-all-done
  31.1 3.9 %reduce-precision_convert_fusion.1.high_ref = bf16[4,512,512]{2,1,0:T(8,128)(2,1)} fusion(f32[1,256,256]{2,1,0:T(8,128)S(1)} %get-tuple-element.36, f32[1,256,256]{2,1,0:T(8,128)} %get-tuple-element.37, f32[1,256,256]{2,1,0:T(8,128)} %get-tuple-element.38, f32[1,256,256]{2,1,0:T(8,128)} %get-tuple-element.39, f32[4,256,256]{2,1,0:T(8,128)S(1)} %maximum_multiply_fusion, ...), kind=kLoop, calls=%fused_computation.3 | loop fusion | flops 14680064 | bytes 5242880 | tf_op jit(solution)/shard_map/convert_element_type | solution.py:21
  35.0 3.1 %fusion.low_ref = bf16[4,512,512]{2,1,0:T(8,128)(2,1)} fusion(f32[1,256,256]{2,1,0:T(8,128)S(1)} %get-tuple-element.36, f32[1,256,256]{2,1,0:T(8,128)S(1)} %copy-done.5, f32[1,256,256]{2,1,0:T(8,128)S(1)} %copy-done.6, f32[1,256,256]{2,1,0:T(8,128)S(1)} %copy-done.7, f32[4,256,256]{2,1,0:T(8,128)S(1)} %maximum_multiply_fusion, ...), kind=kLoop, calls=%fused_computation.4 | loop fusion | flops 15728640 | bytes 5242880 | tf_op jit(solution)/shard_map/convert_element_type | solution.py:21
  38.2 5.8 %shard_map.76 = f32[4,2,256,256]{3,2,1,0:T(8,128)} custom-call(f32[2,1,256,1024]{3,2,1,0:T(8,128)} %field_ref, bf16[4,512,512]{2,1,0:T(8,128)(2,1)} %reduce-precision_convert_fusion.1.high_ref, bf16[4,512,512]{2,1,0:T(8,128)(2,1)} %fusion.low_ref), custom_call_target="tpu_custom_call" | custom-call | tf_op jit(solution)/shard_map/pallas_call | solution.py:238
  44.0 5.1 %all-to-all-start.1 = ((f32[4,2,256,256]{3,2,1,0:T(8,128)}), f32[4,2,256,256]{3,2,1,0:T(8,128)S(1)}, u32[]{:S(2)}, u32[]{:S(2)}) async-start(f32[4,2,256,256]{3,2,1,0:T(8,128)} %shard_map.76), calls=%async_computation.2 | async-start | bytes 4194304 | tf_op jit(solution)/shard_map/all_to_all | solution.py:187
  49.1 11.4 %reduce-scatter.4.cloned.1.call-done = f32[1,256,256]{2,1,0:T(8,128)} async-done(((f32[4,256,256]{2,1,0:T(8,128)}), f32[1,256,256]{2,1,0:T(8,128)}) %reduce-scatter.4.cloned.1.call-update) | async-done | bytes 262160 | tf_op jit(solution)/shard_map/reduce_scatter | solution.py:210
  60.5 5.8 %shard_map.79 = f32[4,2,256,256]{3,2,1,0:T(8,128)} custom-call(f32[2,1,256,1024]{3,2,1,0:T(8,128)} %field_ref.1, bf16[4,512,512]{2,1,0:T(8,128)(2,1)} %reduce-precision_convert_fusion.1.high_ref, bf16[4,512,512]{2,1,0:T(8,128)(2,1)} %fusion.low_ref), custom_call_target="tpu_custom_call" | custom-call | tf_op jit(solution)/shard_map/pallas_call | solution.py:238
  66.3 6.8 %all-to-all-done.1.field_ref = f32[4,2,256,256]{3,2,1,0:T(8,128)S(1)} async-done(((f32[4,2,256,256]{3,2,1,0:T(8,128)}), f32[4,2,256,256]{3,2,1,0:T(8,128)S(1)}, u32[]{:S(2)}, u32[]{:S(2)}) %all-to-all-start.1) | async-done | bytes 2097184 | tf_op jit(solution)/shard_map/all_to_all | solution.py:187
  74.4 5.2 %all-to-all-start.3 = ((f32[4,2,256,256]{3,2,1,0:T(8,128)}), f32[4,2,256,256]{3,2,1,0:T(8,128)S(1)}, u32[]{:S(2)}, u32[]{:S(2)}) async-start(f32[4,2,256,256]{3,2,1,0:T(8,128)} %shard_map.79), calls=%async_computation.4 | async-start | bytes 4194304 | tf_op jit(solution)/shard_map/all_to_all | solution.py:187
  79.7 1.8 broadcast_multiply_fusion
  81.5 2.4 fusion.1
  83.9 4.9 %all-gather.2.cloned.1.call-done = f32[4,256,256]{2,1,0:T(8,128)} async-done(((f32[1,256,256]{2,1,0:T(8,128)}), f32[4,256,256]{2,1,0:T(8,128)}) %all-gather.2.cloned.1.call-update) | async-done | bytes 1048592 | tf_op jit(solution)/shard_map/all_gather | solution.py:212
  88.8 5.7 %multiply_sine_fusion = (f32[4,256,256]{2,1,0:T(8,128)}, f32[4,256,256]{2,1,0:T(8,128)}) fusion(f32[4,256,256]{2,1,0:T(8,128)} %all-gather.2.cloned.1.call-done, f32[]{:T(128)} %bitcast.4), kind=kLoop, calls=%fused_computation.33 | loop fusion | flops 262144 | bytes 3145732 | tf_op jit(solution)/shard_map/sin | solution.py:203
  94.5 9.1 %shard_map.77 = (f32[4,2,256,256]{3,2,1,0:T(8,128)}, f32[4,2,256,256]{3,2,1,0:T(8,128)}) custom-call(f32[4,256,256]{2,1,0:T(8,128)} %get-tuple-element.41.cos_ref, f32[4,256,256]{2,1,0:T(8,128)} %get-tuple-element.40.sin_ref, f32[4,2,256,256]{3,2,1,0:T(8,128)} %copy-done.3, bf16[4,512,512]{2,1,0:T(8,128)(2,1)} %get-tuple-element.28.high_ref, ...), custom_call_target="tpu_custom_call" | custom-call | tf_op jit(solution)/shard_map/pallas_call | solution.py:269
  105.0 6.1 %all-to-all-start.2 = ((f32[4,2,256,256]{3,2,1,0:T(8,128)}), f32[4,2,256,256]{3,2,1,0:T(8,128)}, u32[]{:S(2)}, u32[]{:S(2)}) async-start(f32[4,2,256,256]{3,2,1,0:T(8,128)} %get-tuple-element.20), calls=%async_computation.3 | async-start | bytes 4194304 | tf_op jit(solution)/shard_map/all_to_all | solution.py:187
  111.9 9.8 %shard_map.80 = (f32[4,2,256,256]{3,2,1,0:T(8,128)}, f32[4,256,256]{2,1,0:T(8,128)}) custom-call(f32[4,256,256]{2,1,0:T(8,128)} %get-tuple-element.41.cos_ref, f32[4,256,256]{2,1,0:T(8,128)} %get-tuple-element.40.sin_ref, f32[4,2,256,256]{3,2,1,0:T(8,128)} %copy-done, bf16[4,512,512]{2,1,0:T(8,128)(2,1)} %get-tuple-element.28.high_ref, ...), custom_call_target="tpu_custom_call" | custom-call | tf_op jit(solution)/shard_map/pallas_call | solution.py:278
  121.7 13.5 %all-to-all-done.2.field_ref = f32[4,2,256,256]{3,2,1,0:T(8,128)} async-done(((f32[4,2,256,256]{3,2,1,0:T(8,128)}), f32[4,2,256,256]{3,2,1,0:T(8,128)}, u32[]{:S(2)}, u32[]{:S(2)}) %all-to-all-start.2) | async-done | bytes 2097184 | tf_op jit(solution)/shard_map/all_to_all | solution.py:187
  135.3 5.2 %all-to-all-start.4 = ((f32[4,2,256,256]{3,2,1,0:T(8,128)}), f32[4,2,256,256]{3,2,1,0:T(8,128)S(1)}, u32[]{:S(2)}, u32[]{:S(2)}) async-start(f32[4,2,256,256]{3,2,1,0:T(8,128)} %get-tuple-element.23), calls=%async_computation.5 | async-start | bytes 4194304 | tf_op jit(solution)/shard_map/all_to_all | solution.py:187
  140.5 27.7 %all-reduce.2.cloned.1.call-done = f32[256,1024]{1,0:T(8,128)} async-done(((f32[256,1024]{1,0:T(8,128)}), f32[256,1024]{1,0:T(8,128)}) %all-reduce.2.cloned.1.call-update) | async-done | bytes 1048592 | tf_op jit(solution)/shard_map/psum | solution.py:214
  168.2 5.7 %multiply_sine_fusion.1 = (f32[256,1024]{1,0:T(8,128)}, f32[256,1024]{1,0:T(8,128)}) fusion(f32[256,1024]{1,0:T(8,128)} %all-reduce.2.cloned.1.call-done, f32[]{:T(128)} %bitcast.4), kind=kLoop, calls=%fused_computation.35 | loop fusion | flops 262144 | bytes 3145732 | tf_op jit(solution)/shard_map/sin | solution.py:203
  173.9 6.4 %shard_map.78.source_ref = f32[2,1,256,1024]{3,2,1,0:T(8,128)} custom-call(f32[256,1024]{1,0:T(8,128)} %get-tuple-element.43.cos_ref, f32[256,1024]{1,0:T(8,128)} %get-tuple-element.42.sin_ref, f32[4,2,256,256]{3,2,1,0:T(8,128)} %all-to-all-done.2.field_ref, bf16[4,512,512]{2,1,0:T(8,128)(2,1)} %reduce-precision_convert_fusion.1.high_ref, ...), custom_call_target="tpu_custom_call" | custom-call | tf_op jit(solution)/shard_map/pallas_call | solution.py:301
  180.3 1.4 copy-done.1
  181.7 6.8 %shard_map.81 = (f32[2,1,256,1024]{3,2,1,0:T(8,128)}, f32[256,1024]{1,0:T(8,128)}) custom-call(f32[256,1024]{1,0:T(8,128)} %get-tuple-element.43.cos_ref, f32[256,1024]{1,0:T(8,128)} %get-tuple-element.42.sin_ref, f32[4,2,256,256]{3,2,1,0:T(8,128)} %copy-done.1, bf16[4,512,512]{2,1,0:T(8,128)(2,1)} %reduce-precision_convert_fusion.1.high_ref, ...), custom_call_target="tpu_custom_call" | custom-call | tf_op jit(solution)/shard_map/pallas_call | solution.py:309
  188.5 8.4 %reduce-scatter.6.cloned.1.call-done = f32[256,256]{1,0:T(8,128)} async-done(((f32[1024,256]{1,0:T(8,128)}), f32[256,256]{1,0:T(8,128)}) %reduce-scatter.6.cloned.1.call-update) | async-done | bytes 262160 | tf_op jit(solution)/shard_map/reduce_scatter | solution.py:290
  196.9 2.9 %collective-permute-start = (f32[256,256]{1,0:T(8,128)}, f32[256,256]{1,0:T(8,128)S(1)}, u32[]{:S(2)}, u32[]{:S(2)}) collective-permute-start(f32[256,256]{1,0:T(8,128)} %reduce-scatter.6.cloned.1.call-done), channel_id=1, source_target_pairs={{0,0},{1,4},{2,8},{3,12},{4,1},{5,5},{6,9},{7,13},{8,2},{9,6},{10,... | collective-permute-start | bytes 786440 | tf_op jit(solution)/shard_map/ppermute | solution.py:296
  199.9 27.2 %collective-permute-done = f32[256,256]{1,0:T(8,128)S(1)} collective-permute-done((f32[256,256]{1,0:T(8,128)}, f32[256,256]{1,0:T(8,128)S(1)}, u32[]{:S(2)}, u32[]{:S(2)}) %collective-permute-start) | collective-permute-done | bytes 262176 | tf_op jit(solution)/shard_map/ppermute | solution.py:296
  227.0 2.1 reduce-scatter.8.cloned.1.call-done
  229.2 1.8 pad_maximum_fusion
  (35 shorter events, 9.4 us)
Async XLA Ops:
  13.9 16.1 %all-to-all-start = ((f32[4,256,256]{2,1,0:T(8,128)}), f32[4,256,256]{2,1,0:T(8,128)S(1)}, u32[]{:S(2)}, u32[]{:S(2)}) async-start(f32[4,256,256]{2,1,0:T(8,128)} %bitcast.11), calls=%async_computation | async-start | bytes 2097152 | tf_op jit(solution)/shard_map/all_to_all | solution.py:187
  17.4 43.1 %reduce-scatter.4.cloned.1.call-start = ((), (), s32[]{:S(2)}) async-start(), calls=%async_computation.8 | async-start | bytes 1310720 | tf_op jit(solution)/shard_map/reduce_scatter | solution.py:210
  26.3 1.6 copy-start.2
  30.0 1.0 copy-start.4
  31.1 4.0 %copy-start.5 = (f32[1,256,256]{2,1,0:T(8,128)S(1)}, f32[1,256,256]{2,1,0:T(8,128)}, u32[]{:S(2)}) copy-start(f32[1,256,256]{2,1,0:T(8,128)} %get-tuple-element.37) | copy-start | bytes 786436
  31.1 3.9 %copy-start.6 = (f32[1,256,256]{2,1,0:T(8,128)S(1)}, f32[1,256,256]{2,1,0:T(8,128)}, u32[]{:S(2)}) copy-start(f32[1,256,256]{2,1,0:T(8,128)} %get-tuple-element.38) | copy-start | bytes 786436
  31.1 3.9 %copy-start.7 = (f32[1,256,256]{2,1,0:T(8,128)S(1)}, f32[1,256,256]{2,1,0:T(8,128)}, u32[]{:S(2)}) copy-start(f32[1,256,256]{2,1,0:T(8,128)} %get-tuple-element.39) | copy-start | bytes 786436
  44.0 29.1 %all-to-all-start.1 = ((f32[4,2,256,256]{3,2,1,0:T(8,128)}), f32[4,2,256,256]{3,2,1,0:T(8,128)S(1)}, u32[]{:S(2)}, u32[]{:S(2)}) async-start(f32[4,2,256,256]{3,2,1,0:T(8,128)} %shard_map.76), calls=%async_computation.2 | async-start | bytes 4194304 | tf_op jit(solution)/shard_map/all_to_all | solution.py:187
  49.1 39.7 %all-gather.2.cloned.1.call-start = ((), (), s32[]{:S(2)}) async-start(), calls=%async_computation.9 | async-start | bytes 1310720 | tf_op jit(solution)/shard_map/all_gather | solution.py:212
  73.1 1.3 copy-start.3
  74.4 29.3 %all-to-all-start.3 = ((f32[4,2,256,256]{3,2,1,0:T(8,128)}), f32[4,2,256,256]{3,2,1,0:T(8,128)S(1)}, u32[]{:S(2)}, u32[]{:S(2)}) async-start(f32[4,2,256,256]{3,2,1,0:T(8,128)} %shard_map.79), calls=%async_computation.4 | async-start | bytes 4194304 | tf_op jit(solution)/shard_map/all_to_all | solution.py:187
  103.7 1.3 copy-start
  105.0 30.2 %all-to-all-start.2 = ((f32[4,2,256,256]{3,2,1,0:T(8,128)}), f32[4,2,256,256]{3,2,1,0:T(8,128)}, u32[]{:S(2)}, u32[]{:S(2)}) async-start(f32[4,2,256,256]{3,2,1,0:T(8,128)} %get-tuple-element.20), calls=%async_computation.3 | async-start | bytes 4194304 | tf_op jit(solution)/shard_map/all_to_all | solution.py:187
  111.1 57.1 %all-reduce.2.cloned.1.call-start = ((), (), s32[]{:S(2)}) async-start(), calls=%async_computation.10 | async-start | bytes 2097152 | tf_op jit(solution)/shard_map/psum | solution.py:214
  111.8 85.1 %reduce-scatter.6.cloned.1.call-start = ((), (), s32[]{:S(2)}) async-start(), calls=%async_computation.11 | async-start | bytes 1310720 | tf_op jit(solution)/shard_map/reduce_scatter | solution.py:290
  135.3 45.0 %all-to-all-start.4 = ((f32[4,2,256,256]{3,2,1,0:T(8,128)}), f32[4,2,256,256]{3,2,1,0:T(8,128)S(1)}, u32[]{:S(2)}, u32[]{:S(2)}) async-start(f32[4,2,256,256]{3,2,1,0:T(8,128)} %get-tuple-element.23), calls=%async_computation.5 | async-start | bytes 4194304 | tf_op jit(solution)/shard_map/all_to_all | solution.py:187
  140.5 88.7 %reduce-scatter.8.cloned.1.call-start = ((), (), s32[]{:S(2)}) async-start(), calls=%async_computation.12 | async-start | bytes 1310720 | tf_op jit(solution)/shard_map/reduce_scatter | solution.py:317
  180.3 1.4 copy-start.1
  196.9 30.1 %collective-permute-start = (f32[256,256]{1,0:T(8,128)}, f32[256,256]{1,0:T(8,128)S(1)}, u32[]{:S(2)}, u32[]{:S(2)}) collective-permute-start(f32[256,256]{1,0:T(8,128)} %reduce-scatter.6.cloned.1.call-done), channel_id=1, source_target_pairs={{0,0},{1,4},{2,8},{3,12},{4,1},{5,5},{6,9},{7,13},{8,2},{9,6},{10,... | collective-permute-start | bytes 786440 | tf_op jit(solution)/shard_map/ppermute | solution.py:296
Sparse Core Ops, SparseCore 0:
  31.2 29.2 reduce-scatter.3
  62.2 26.5 all-gather.1
  114.4 53.7 all-reduce.1
  170.4 26.5 reduce-scatter.5
  199.2 29.9 reduce-scatter.7

commit v3 on v2

--- a/solution.py
+++ b/solution.py
@@ -206,14 +206,15 @@
         return jnp.where(lax.axis_index("freq") == owner[depth], slowness[0], 0.0)
 
     turned = swap(jnp.moveaxis(owned(0).reshape(rows, row_count, cols), 1, 0))
+    piece_last = lax.psum_scatter(owned(1), "freq", scatter_dimension=0, tiled=True)
     source_field, turned = lax.optimization_barrier((source_field, turned))
+    turned, piece_last = lax.optimization_barrier((turned, piece_last))
     piece = lax.psum_scatter(turned, "freq", scatter_dimension=0, tiled=True)
     receiver_field, piece = lax.optimization_barrier((receiver_field, piece))
     slab_first = lax.all_gather(piece, "freq", axis=0, tiled=True)
-    slab, slab_first = lax.optimization_barrier((owned(1), slab_first))
-    slab_last = lax.psum(slab, "freq")
+    piece_last, slab_first = lax.optimization_barrier((piece_last, slab_first))
+    slab_last = lax.all_gather(piece_last, "freq", axis=0, tiled=True)
     turn_first = turning(slab_first.reshape(4, quart_h, cols))
-    turn_last = turning(slab_last)
 
     block_w = toeplitz_blocks(width, omega[0])
     block_h = block_w if height == width else toeplitz_blocks(height, omega[0])
@@ -283,6 +284,8 @@
         out_shape=[col_shape, term_shape],
         compiler_params=params(),
     )(*turn_first, receiver, col_high, col_low, middle)
+    receiver, term, slab_last = lax.optimization_barrier((receiver, term, slab_last))
+    turn_last = turning(slab_last)
     receiver = to_rows(receiver)
 
     term = term.reshape(height, cols)

time: 241 us -> 229 us (0.950)
  waiting for transfers between devices: 105 us -> 93.6 us
    psum x1 -> x0, waiting for transfers between devices: 27.7 us -> none  [body(): slab_last = lax.psum(slab, 'freq')]
    all_to_all x5, waiting for transfers between devices: 22.6 us -> 36.5 us  [swap(): lax.all_to_all(blocks, 'row', split_axis=0, concat_axis=0, tiled=True)]
    reduce_scatter x0 -> x1, waiting for transfers between devices: none -> 10.8 us  [body(): lax.psum_scatter(owned(1), 'freq', scatter_dimension=0, tiled=True)]
    reduce_scatter x1, waiting for transfers between devices: 8.43 us -> 0.02 us  [body(): part = lax.psum_scatter(term, 'freq', scatter_dimension=0, tiled=True)]
    unnamed x16 -> x20, local copies, waits for them, and re-layouts: 5.42 us -> 4.43 us
  transfers between devices with their start and end apart: 11 -> 12, of which waited for: 10 -> 9; matrix products, arithmetic and copies ran while one was open for 13% -> 15% of each run, Pallas kernels for 18% -> 19%
where the time goes in v3:
time: 229 us; the launch traced here: 225 us
  waiting for transfers between devices  93.6 us (41%)
  Pallas kernels  43.4 us (19%)
  other arithmetic  31.8 us (14%)
  starting transfers between devices  28.1 us (12%)
  between operations  16.2 us (7%)
  local copies, waits for them, and re-layouts  8.6 us (4%)
  matrix products  3.71 us (2%)
    all_to_all x5, waiting for transfers between devices, swap(): lax.all_to_all(blocks, 'row', split_axis=0, concat_axis=0, tiled=True)  36.5 us
    ppermute x1, waiting for transfers between devices, body(): image_first = lax.ppermute(part, ('row', 'freq'), pairs)  27.1 us
    all_to_all x5, starting transfers between devices, swap(): lax.all_to_all(blocks, 'row', split_axis=0, concat_axis=0, tiled=True)  23 us
    pallas_call x2, Pallas kernels, first(): pl.pallas_call(partial(first_kernel, sign), grid=(rows // step,), in_spec...  11.4 us
    reduce_scatter x1, waiting for transfers between devices, body(): piece = lax.psum_scatter(turned, 'freq', scatter_dimension=0, tiled=True)  11.3 us
    convert_element_type x3, other arithmetic, split_high_low(): return (high.astype(jnp.bfloat16), (value - high).astype(jnp.bfloat16))  10.9 us
    reduce_scatter x1, waiting for transfers between devices, body(): lax.psum_scatter(owned(1), 'freq', scatter_dimension=0, tiled=True)  10.8 us
    pallas_call x1, Pallas kernels, body(): pl.pallas_call(middle_receiver, grid=(1,), in_specs=[term_block, term_blo...  9.85 us
  transfers between devices with their start and end apart: 12, of which 9 were waited for; matrix products, arithmetic and copies ran while one was open for 15% of the time, Pallas kernels for 19%

profile of v3, /device:TPU:2, one launch (start us, length us, event | category | flops | bytes accessed | tf_op | source)
XLA Modules:
  0.0 225.5 jit_solution(8459430203313225775)
XLA Ops:
  9.8 2.5 %select_bitcast_fusion = (f32[256,1024]{1,0:T(8,128)}, f32[1,256,1024]{2,1,0:T(8,128)S(1)}) fusion(f32[1,256,1024]{2,1,0:T(8,128)} %param.7, pred[]{:T(512)S(6)} %eq.9, pred[]{:T(512)S(6)} %eq.8), kind=kLoop, calls=%fused_computation.31 | loop fusion | flops 524288 | bytes 3145730 | tf_op jit(solution)/shard_map/jit(_where)/select_n | solution.py:206
  14.0 3.5 %all-to-all-start = ((f32[4,256,256]{2,1,0:T(8,128)}), f32[4,256,256]{2,1,0:T(8,128)S(1)}, u32[]{:S(2)}, u32[]{:S(2)}) async-start(f32[4,256,256]{2,1,0:T(8,128)} %bitcast.11), calls=%async_computation | async-start | bytes 2097152 | tf_op jit(solution)/shard_map/all_to_all | solution.py:187
  18.3 4.3 %multiply_subtract_fusion = (f32[4,256,256]{2,1,0:T(8,128)S(1)}, f32[4,256,256]{2,1,0:T(8,128)S(1)}, f32[4,256,256]{2,1,0:T(8,128)S(1)}, f32[4,256,256]{2,1,0:T(8,128)S(1)}, f32[4,256,256]{2,1,0:T(8,128)S(1)}) fusion(f32[4,256]{1,0:T(4,128)S(1)} %get-tuple-element.62, f32[4,256]{1,0:T(4,128)S(1)} %get-tuple-element.61, s32[4,256]{1,0:T(4,128)S(1)} %iota_add_fusion), kind=kLoop, calls=%fused_computation.28 | loop fusion | flops 5505024 | bytes 5255168 | tf_op jit(solution)/shard_map/sub | solution.py:39
  22.6 3.7 %fusion.2 = f32[4,256,512]{2,1,0:T(8,128)S(1)} fusion(f32[4,256,256]{2,1,0:T(8,128)S(1)} %get-tuple-element.60, f32[4,256,256]{2,1,0:T(8,128)S(1)} %get-tuple-element.59, f32[4,256,256]{2,1,0:T(8,128)S(1)} %get-tuple-element.58, f32[4,256,256]{2,1,0:T(8,128)S(1)} %get-tuple-element.57, f32[4,256,256]{2,1,0:T(8,128)S(1)} %get-tuple-element.56), kind=kOutput, calls=%fused_computation.6 | convolution fusion | flops 3224895488 | bytes 7340032 | tf_op jit(solution)/shard_map/kbm,kcm->kbc/dot_general | solution.py:43
  28.0 2.1 all-to-all-done
  30.1 10.8 %reduce-scatter.5.cloned.1.call-done = f32[64,1024]{1,0:T(8,128)} async-done(((f32[256,1024]{1,0:T(8,128)}), f32[64,1024]{1,0:T(8,128)}) %reduce-scatter.5.cloned.1.call-update) | async-done | bytes 262160 | tf_op jit(solution)/shard_map/reduce_scatter | solution.py:209
  40.9 3.9 %reduce-precision_convert_fusion.1.high_ref = bf16[4,512,512]{2,1,0:T(8,128)(2,1)} fusion(f32[1,256,256]{2,1,0:T(8,128)S(1)} %get-tuple-element.46, f32[1,256,256]{2,1,0:T(8,128)} %get-tuple-element.47, f32[1,256,256]{2,1,0:T(8,128)} %get-tuple-element.48, f32[1,256,256]{2,1,0:T(8,128)} %get-tuple-element.49, f32[4,256,256]{2,1,0:T(8,128)S(1)} %maximum_multiply_fusion, ...), kind=kLoop, calls=%fused_computation.3 | loop fusion | flops 14680064 | bytes 5242880 | tf_op jit(solution)/shard_map/convert_element_type | solution.py:21
  44.9 3.1 %fusion.low_ref = bf16[4,512,512]{2,1,0:T(8,128)(2,1)} fusion(f32[1,256,256]{2,1,0:T(8,128)S(1)} %get-tuple-element.46, f32[1,256,256]{2,1,0:T(8,128)S(1)} %copy-done.5, f32[1,256,256]{2,1,0:T(8,128)S(1)} %copy-done.6, f32[1,256,256]{2,1,0:T(8,128)S(1)} %copy-done.7, f32[4,256,256]{2,1,0:T(8,128)S(1)} %maximum_multiply_fusion, ...), kind=kLoop, calls=%fused_computation.4 | loop fusion | flops 15728640 | bytes 5242880 | tf_op jit(solution)/shard_map/convert_element_type | solution.py:21
  48.0 5.7 %shard_map.77 = f32[4,2,256,256]{3,2,1,0:T(8,128)} custom-call(f32[2,1,256,1024]{3,2,1,0:T(8,128)} %field_ref.1, bf16[4,512,512]{2,1,0:T(8,128)(2,1)} %reduce-precision_convert_fusion.1.high_ref, bf16[4,512,512]{2,1,0:T(8,128)(2,1)} %fusion.low_ref), custom_call_target="tpu_custom_call" | custom-call | tf_op jit(solution)/shard_map/pallas_call | solution.py:239
  53.6 4.1 %all-to-all-start.2 = ((f32[4,2,256,256]{3,2,1,0:T(8,128)}), f32[4,2,256,256]{3,2,1,0:T(8,128)S(1)}, u32[]{:S(2)}, u32[]{:S(2)}) async-start(f32[4,2,256,256]{3,2,1,0:T(8,128)} %shard_map.77), calls=%async_computation.4 | async-start | bytes 4194304 | tf_op jit(solution)/shard_map/all_to_all | solution.py:187
  57.7 11.3 %reduce-scatter.7.cloned.1.call-done = f32[1,256,256]{2,1,0:T(8,128)} async-done(((f32[4,256,256]{2,1,0:T(8,128)}), f32[1,256,256]{2,1,0:T(8,128)}) %reduce-scatter.7.cloned.1.call-update) | async-done | bytes 262160 | tf_op jit(solution)/shard_map/reduce_scatter | solution.py:212
  69.1 5.7 %shard_map.76 = f32[4,2,256,256]{3,2,1,0:T(8,128)} custom-call(f32[2,1,256,1024]{3,2,1,0:T(8,128)} %field_ref, bf16[4,512,512]{2,1,0:T(8,128)(2,1)} %reduce-precision_convert_fusion.1.high_ref, bf16[4,512,512]{2,1,0:T(8,128)(2,1)} %fusion.low_ref), custom_call_target="tpu_custom_call" | custom-call | tf_op jit(solution)/shard_map/pallas_call | solution.py:239
  74.8 7.0 %all-to-all-done.2.field_ref = f32[4,2,256,256]{3,2,1,0:T(8,128)S(1)} async-done(((f32[4,2,256,256]{3,2,1,0:T(8,128)}), f32[4,2,256,256]{3,2,1,0:T(8,128)S(1)}, u32[]{:S(2)}, u32[]{:S(2)}) %all-to-all-start.2) | async-done | bytes 2097184 | tf_op jit(solution)/shard_map/all_to_all | solution.py:187
  83.1 5.2 %all-to-all-start.1 = ((f32[4,2,256,256]{3,2,1,0:T(8,128)}), f32[4,2,256,256]{3,2,1,0:T(8,128)S(1)}, u32[]{:S(2)}, u32[]{:S(2)}) async-start(f32[4,2,256,256]{3,2,1,0:T(8,128)} %shard_map.76), calls=%async_computation.3 | async-start | bytes 4194304 | tf_op jit(solution)/shard_map/all_to_all | solution.py:187
  88.3 3.2 %broadcast_multiply_fusion = (f32[4,256,256]{2,1,0:T(8,128)S(1)}, f32[4,256,256]{2,1,0:T(8,128)}, f32[4,256,256]{2,1,0:T(8,128)}) fusion(f32[4,256,512]{2,1,0:T(8,128)} %copy-done.2), kind=kLoop, calls=%fused_computation.38 | loop fusion | flops 262144 | bytes 5242880 | tf_op jit(solution)/shard_map/mul | solution.py:48
  91.5 5.8 %all-gather.3.cloned.1.call-done = f32[4,256,256]{2,1,0:T(8,128)} async-done(((f32[1,256,256]{2,1,0:T(8,128)}), f32[4,256,256]{2,1,0:T(8,128)}) %all-gather.3.cloned.1.call-update) | async-done | bytes 1048592 | tf_op jit(solution)/shard_map/all_gather | solution.py:214
  97.3 3.8 %fusion.1 = (bf16[4,512,512]{2,1,0:T(8,128)(2,1)}, bf16[4,512,512]{2,1,0:T(8,128)(2,1)}) fusion(f32[4,256,256]{2,1,0:T(8,128)} %get-tuple-element.41, f32[4,256,256]{2,1,0:T(8,128)} %get-tuple-element.40, f32[4,256,256]{2,1,0:T(8,128)S(1)} %get-tuple-element.39), kind=kLoop, calls=%fused_computation.5 | loop fusion | flops 7340032 | bytes 7340032 | tf_op jit(solution)/shard_map/convert_element_type | solution.py:21
  101.1 4.6 %multiply_sine_fusion.1 = (f32[4,256,256]{2,1,0:T(8,128)}, f32[4,256,256]{2,1,0:T(8,128)}) fusion(f32[4,256,256]{2,1,0:T(8,128)S(1)} %copy-done.9, f32[]{:T(128)} %bitcast.4), kind=kLoop, calls=%fused_computation.35 | loop fusion | flops 262144 | bytes 3145732 | tf_op jit(solution)/shard_map/sin | solution.py:203
  105.7 9.2 %shard_map.78 = (f32[4,2,256,256]{3,2,1,0:T(8,128)}, f32[4,2,256,256]{3,2,1,0:T(8,128)}) custom-call(f32[4,256,256]{2,1,0:T(8,128)} %get-tuple-element.53.cos_ref, f32[4,256,256]{2,1,0:T(8,128)} %get-tuple-element.52.sin_ref, f32[4,2,256,256]{3,2,1,0:T(8,128)} %copy-done.3, bf16[4,512,512]{2,1,0:T(8,128)(2,1)} %get-tuple-element.38.high_ref, ...), custom_call_target="tpu_custom_call" | custom-call | tf_op jit(solution)/shard_map/pallas_call | solution.py:270
  116.2 4.9 %all-to-all-start.3 = ((f32[4,2,256,256]{3,2,1,0:T(8,128)}), f32[4,2,256,256]{3,2,1,0:T(8,128)}, u32[]{:S(2)}, u32[]{:S(2)}) async-start(f32[4,2,256,256]{3,2,1,0:T(8,128)} %get-tuple-element.32), calls=%async_computation.5 | async-start | bytes 4194304 | tf_op jit(solution)/shard_map/all_to_all | solution.py:187
  121.1 9.9 %shard_map.79 = (f32[4,2,256,256]{3,2,1,0:T(8,128)}, f32[4,256,256]{2,1,0:T(8,128)}) custom-call(f32[4,256,256]{2,1,0:T(8,128)} %get-tuple-element.53.cos_ref, f32[4,256,256]{2,1,0:T(8,128)} %get-tuple-element.52.sin_ref, f32[4,2,256,256]{3,2,1,0:T(8,128)} %copy-done, bf16[4,512,512]{2,1,0:T(8,128)(2,1)} %get-tuple-element.38.high_ref, ...), custom_call_target="tpu_custom_call" | custom-call | tf_op jit(solution)/shard_map/pallas_call | solution.py:279
  131.0 14.2 %all-to-all-done.3.field_ref = f32[4,2,256,256]{3,2,1,0:T(8,128)} async-done(((f32[4,2,256,256]{3,2,1,0:T(8,128)}), f32[4,2,256,256]{3,2,1,0:T(8,128)}, u32[]{:S(2)}, u32[]{:S(2)}) %all-to-all-start.3) | async-done | bytes 2097184 | tf_op jit(solution)/shard_map/all_to_all | solution.py:187
  145.3 5.2 %all-to-all-start.4 = ((f32[4,2,256,256]{3,2,1,0:T(8,128)}), f32[4,2,256,256]{3,2,1,0:T(8,128)S(1)}, u32[]{:S(2)}, u32[]{:S(2)}) async-start(f32[4,2,256,256]{3,2,1,0:T(8,128)} %get-tuple-element.33), calls=%async_computation.6 | async-start | bytes 4194304 | tf_op jit(solution)/shard_map/all_to_all | solution.py:187
  150.5 4.5 %multiply_sine_fusion = (f32[256,1024]{1,0:T(8,128)}, f32[256,1024]{1,0:T(8,128)}) fusion(f32[256,1024]{1,0:T(8,128)S(1)} %copy-done.8, f32[]{:T(128)} %bitcast.4), kind=kLoop, calls=%fused_computation.33 | loop fusion | flops 262144 | bytes 3145732 | tf_op jit(solution)/shard_map/sin | solution.py:203
  155.0 6.2 %shard_map.80.source_ref = f32[2,1,256,1024]{3,2,1,0:T(8,128)} custom-call(f32[256,1024]{1,0:T(8,128)} %get-tuple-element.51.cos_ref, f32[256,1024]{1,0:T(8,128)} %get-tuple-element.50.sin_ref, f32[4,2,256,256]{3,2,1,0:T(8,128)} %all-to-all-done.3.field_ref, bf16[4,512,512]{2,1,0:T(8,128)(2,1)} %reduce-precision_convert_fusion.1.high_ref, ...), custom_call_target="tpu_custom_call" | custom-call | tf_op jit(solution)/shard_map/pallas_call | solution.py:304
  161.3 13.3 %all-to-all-done.4.field_ref = f32[4,2,256,256]{3,2,1,0:T(8,128)S(1)} async-done(((f32[4,2,256,256]{3,2,1,0:T(8,128)}), f32[4,2,256,256]{3,2,1,0:T(8,128)S(1)}, u32[]{:S(2)}, u32[]{:S(2)}) %all-to-all-start.4) | async-done | bytes 2097184 | tf_op jit(solution)/shard_map/all_to_all | solution.py:187
  174.5 1.4 copy-done.1
  175.9 6.8 %shard_map.81 = (f32[2,1,256,1024]{3,2,1,0:T(8,128)}, f32[256,1024]{1,0:T(8,128)}) custom-call(f32[256,1024]{1,0:T(8,128)} %get-tuple-element.51.cos_ref, f32[256,1024]{1,0:T(8,128)} %get-tuple-element.50.sin_ref, f32[4,2,256,256]{3,2,1,0:T(8,128)} %copy-done.1, bf16[4,512,512]{2,1,0:T(8,128)(2,1)} %reduce-precision_convert_fusion.1.high_ref, ...), custom_call_target="tpu_custom_call" | custom-call | tf_op jit(solution)/shard_map/pallas_call | solution.py:312
  182.8 5.0 %collective-permute-start = (f32[256,256]{1,0:T(8,128)}, f32[256,256]{1,0:T(8,128)S(1)}, u32[]{:S(2)}, u32[]{:S(2)}) collective-permute-start(f32[256,256]{1,0:T(8,128)} %reduce-scatter.9.cloned.1.call-done), channel_id=1, source_target_pairs={{0,0},{1,4},{2,8},{3,12},{4,1},{5,5},{6,9},{7,13},{8,2},{9,6},{10,... | collective-permute-start | bytes 786440 | tf_op jit(solution)/shard_map/ppermute | solution.py:299
  187.8 27.1 %collective-permute-done = f32[256,256]{1,0:T(8,128)S(1)} collective-permute-done((f32[256,256]{1,0:T(8,128)}, f32[256,256]{1,0:T(8,128)S(1)}, u32[]{:S(2)}, u32[]{:S(2)}) %collective-permute-start) | collective-permute-done | bytes 262176 | tf_op jit(solution)/shard_map/ppermute | solution.py:299
  214.9 1.9 reduce-scatter.11.cloned.1.call-done
  216.9 1.8 pad_maximum_fusion
  (42 shorter events, 7.6 us)
Async XLA Ops:
  7.2 33.7 %reduce-scatter.5.cloned.1.call-start = ((), (), s32[]{:S(2)}) async-start(), calls=%async_computation.9 | async-start | bytes 1310720 | tf_op jit(solution)/shard_map/reduce_scatter | solution.py:209
  14.0 16.1 %all-to-all-start = ((f32[4,256,256]{2,1,0:T(8,128)}), f32[4,256,256]{2,1,0:T(8,128)S(1)}, u32[]{:S(2)}, u32[]{:S(2)}) async-start(f32[4,256,256]{2,1,0:T(8,128)} %bitcast.11), calls=%async_computation | async-start | bytes 2097152 | tf_op jit(solution)/shard_map/all_to_all | solution.py:187
  17.5 51.6 %reduce-scatter.7.cloned.1.call-start = ((), (), s32[]{:S(2)}) async-start(), calls=%async_computation.10 | async-start | bytes 1310720 | tf_op jit(solution)/shard_map/reduce_scatter | solution.py:212
  26.4 1.6 copy-start.2
  30.1 10.8 %copy-start.4 = (f32[4,256,256]{2,1,0:T(8,128)}, f32[4,256,256]{2,1,0:T(8,128)S(1)}, u32[]{:S(2)}) copy-start(f32[4,256,256]{2,1,0:T(8,128)S(1)} %all-to-all-done) | copy-start | bytes 3145732
  40.9 4.0 %copy-start.5 = (f32[1,256,256]{2,1,0:T(8,128)S(1)}, f32[1,256,256]{2,1,0:T(8,128)}, u32[]{:S(2)}) copy-start(f32[1,256,256]{2,1,0:T(8,128)} %get-tuple-element.47) | copy-start | bytes 786436
  40.9 4.0 %copy-start.6 = (f32[1,256,256]{2,1,0:T(8,128)S(1)}, f32[1,256,256]{2,1,0:T(8,128)}, u32[]{:S(2)}) copy-start(f32[1,256,256]{2,1,0:T(8,128)} %get-tuple-element.48) | copy-start | bytes 786436
  40.9 3.9 %copy-start.7 = (f32[1,256,256]{2,1,0:T(8,128)S(1)}, f32[1,256,256]{2,1,0:T(8,128)}, u32[]{:S(2)}) copy-start(f32[1,256,256]{2,1,0:T(8,128)} %get-tuple-element.49) | copy-start | bytes 786436
  53.6 28.1 %all-to-all-start.2 = ((f32[4,2,256,256]{3,2,1,0:T(8,128)}), f32[4,2,256,256]{3,2,1,0:T(8,128)S(1)}, u32[]{:S(2)}, u32[]{:S(2)}) async-start(f32[4,2,256,256]{3,2,1,0:T(8,128)} %shard_map.77), calls=%async_computation.4 | async-start | bytes 4194304 | tf_op jit(solution)/shard_map/all_to_all | solution.py:187
  57.7 39.5 %all-gather.3.cloned.1.call-start = ((), (), s32[]{:S(2)}) async-start(), calls=%async_computation.11 | async-start | bytes 1310720 | tf_op jit(solution)/shard_map/all_gather | solution.py:214
  81.8 1.3 copy-start.3
  83.1 31.8 %all-to-all-start.1 = ((f32[4,2,256,256]{3,2,1,0:T(8,128)}), f32[4,2,256,256]{3,2,1,0:T(8,128)S(1)}, u32[]{:S(2)}, u32[]{:S(2)}) async-start(f32[4,2,256,256]{3,2,1,0:T(8,128)} %shard_map.76), calls=%async_computation.3 | async-start | bytes 4194304 | tf_op jit(solution)/shard_map/all_to_all | solution.py:187
  88.3 42.6 %all-gather.5.cloned.1.call-start = ((), (), s32[]{:S(2)}) async-start(), calls=%async_computation.12 | async-start | bytes 1310720 | tf_op jit(solution)/shard_map/all_gather | solution.py:216
  97.3 3.8 %copy-start.9 = (f32[4,256,256]{2,1,0:T(8,128)S(1)}, f32[4,256,256]{2,1,0:T(8,128)}, u32[]{:S(2)}) copy-start(f32[4,256,256]{2,1,0:T(8,128)} %all-gather.3.cloned.1.call-done) | copy-start | bytes 3145732
  114.9 1.3 copy-start
  116.2 29.1 %all-to-all-start.3 = ((f32[4,2,256,256]{3,2,1,0:T(8,128)}), f32[4,2,256,256]{3,2,1,0:T(8,128)}, u32[]{:S(2)}, u32[]{:S(2)}) async-start(f32[4,2,256,256]{3,2,1,0:T(8,128)} %get-tuple-element.32), calls=%async_computation.5 | async-start | bytes 4194304 | tf_op jit(solution)/shard_map/all_to_all | solution.py:187
  121.1 61.6 %reduce-scatter.9.cloned.1.call-start = ((), (), s32[]{:S(2)}) async-start(), calls=%async_computation.13 | async-start | bytes 1310720 | tf_op jit(solution)/shard_map/reduce_scatter | solution.py:293
  131.0 19.5 %copy-start.8 = (f32[256,1024]{1,0:T(8,128)S(1)}, f32[256,1024]{1,0:T(8,128)}, u32[]{:S(2)}) copy-start(f32[256,1024]{1,0:T(8,128)} %all-gather.5.cloned.1.call-done) | copy-start | bytes 3145732
  145.3 29.3 %all-to-all-start.4 = ((f32[4,2,256,256]{3,2,1,0:T(8,128)}), f32[4,2,256,256]{3,2,1,0:T(8,128)S(1)}, u32[]{:S(2)}, u32[]{:S(2)}) async-start(f32[4,2,256,256]{3,2,1,0:T(8,128)} %get-tuple-element.33), calls=%async_computation.6 | async-start | bytes 4194304 | tf_op jit(solution)/shard_map/all_to_all | solution.py:187
  150.5 66.4 %reduce-scatter.11.cloned.1.call-start = ((), (), s32[]{:S(2)}) async-start(), calls=%async_computation.14 | async-start | bytes 1310720 | tf_op jit(solution)/shard_map/reduce_scatter | solution.py:320
  174.5 1.4 copy-start.1
  182.8 32.2 %collective-permute-start = (f32[256,256]{1,0:T(8,128)}, f32[256,256]{1,0:T(8,128)S(1)}, u32[]{:S(2)}, u32[]{:S(2)}) collective-permute-start(f32[256,256]{1,0:T(8,128)} %reduce-scatter.9.cloned.1.call-done), channel_id=1, source_target_pairs={{0,0},{1,4},{2,8},{3,12},{4,1},{5,5},{6,9},{7,13},{8,2},{9,6},{10,... | collective-permute-start | bytes 786440 | tf_op jit(solution)/shard_map/ppermute | solution.py:299
Sparse Core Ops, SparseCore 0:
  12.4 28.3 reduce-scatter.4
  43.2 25.7 reduce-scatter.6
  70.6 26.5 all-gather.2
  98.7 27.4 all-gather.4
  131.1 26.7 reduce-scatter.8
  182.8 33.9 reduce-scatter.10

commit v4 on v3

--- a/solution.py
+++ b/solution.py
@@ -168,7 +168,9 @@
 
 def last_receiver(cos_ref, sin_ref, field_ref, high_ref, low_ref, source_ref, receiver_ref, term_ref):
     def keep(span, re, im):
-        term_ref[:, span] = source_ref[0, 0, :, span] * re - source_ref[1, 0, :, span] * im
+        term_ref[span.start // span.size] = (
+            source_ref[0, 0, :, span] * re - source_ref[1, 0, :, span] * im
+        )
         receiver_ref[0, 0, :, span] = re
         receiver_ref[1, 0, :, span] = -im
 
@@ -185,6 +187,16 @@
 
 def swap(blocks):
     return lax.all_to_all(blocks, "row", split_axis=0, concat_axis=0, tiled=True)
+
+
+def sum_strips(strips):
+    count = strips.shape[0]
+    me = lax.axis_index("freq")
+    total = lax.dynamic_index_in_dim(strips, me, 0, keepdims=False)
+    for shift in range(1, count):
+        sent = lax.dynamic_index_in_dim(strips, (me + shift) % count, 0, keepdims=False)
+        total = total + lax.ppermute(sent, "freq", [(i, (i + shift) % count) for i in range(count)])
+    return total
 
 
 def body(source_field, receiver_field, slowness, owner, freq_index):
@@ -232,7 +244,8 @@
     quarter_shape = jax.ShapeDtypeStruct((4, 2, rows, quart_w), jnp.float32)
     col_shape = jax.ShapeDtypeStruct((4, 2, quart_h, cols), jnp.float32)
     term_shape = jax.ShapeDtypeStruct((4, quart_h, cols), jnp.float32)
-    line_shape = jax.ShapeDtypeStruct((rows, width), jnp.float32)
+    strip_block = pl.BlockSpec((4, step, quart_w), lambda i: (0, i, 0))
+    strip_shape = jax.ShapeDtypeStruct((4, rows, quart_w), jnp.float32)
     field_shape = jax.ShapeDtypeStruct(source_field.shape, jnp.float32)
 
     def first(field, sign):
@@ -313,11 +326,15 @@
         last_receiver,
         grid=(rows // step,),
         in_specs=[line_block, line_block, quarter_block, mat_w, mat_w, row_block],
-        out_specs=[row_block, line_block],
-        out_shape=[field_shape, line_shape],
+        out_specs=[row_block, strip_block],
+        out_shape=[field_shape, strip_shape],
         compiler_params=params(),
     )(*turn_last, receiver, row_high, row_low, source_out)
-    image_last = lax.psum_scatter(term, "freq", scatter_dimension=1, tiled=True)
+    if freq_count == 4:
+        image_last = sum_strips(term)
+    else:
+        term = jnp.moveaxis(term, 0, 1).reshape(rows, width)
+        image_last = lax.psum_scatter(term, "freq", scatter_dimension=1, tiled=True)
     return source_out, receiver_out, jnp.stack([image_first, image_last])
 
 

time: 229 us -> 228 us (level)
  starting transfers between devices: 28.1 us -> 33.2 us
    ppermute x0 -> x3, waiting for transfers between devices: none -> 12.3 us  [sum_strips(): lax.ppermute(sent, 'freq', [(i, (i + shift) % count) for i in range(count)])]
    ppermute x1, waiting for transfers between devices: 27.1 us -> 15.9 us  [body(): image_first = lax.ppermute(part, ('row', 'freq'), pairs)]
    ppermute x0 -> x3, starting transfers between devices: none -> 4.19 us  [sum_strips(): lax.ppermute(sent, 'freq', [(i, (i + shift) % count) for i in range(count)])]
  transfers between devices with their start and end apart: 12 -> 14, of which waited for: 9 -> 11; matrix products, arithmetic and copies ran while one was open for 15% -> 15% of each run, Pallas kernels for 19% -> 19%
where the time goes in v4:
time: 228 us; the launch traced here: 227 us
  waiting for transfers between devices  91.8 us (40%)
  Pallas kernels  43.6 us (19%)
  starting transfers between devices  33.2 us (15%)
  other arithmetic  30.2 us (13%)
  between operations  15.9 us (7%)
  local copies, waits for them, and re-layouts  8.39 us (4%)
  matrix products  3.71 us (2%)
    all_to_all x5, waiting for transfers between devices, swap(): lax.all_to_all(blocks, 'row', split_axis=0, concat_axis=0, tiled=True)  36.6 us
    all_to_all x5, starting transfers between devices, swap(): lax.all_to_all(blocks, 'row', split_axis=0, concat_axis=0, tiled=True)  24.2 us
    ppermute x1, waiting for transfers between devices, body(): image_first = lax.ppermute(part, ('row', 'freq'), pairs)  15.9 us
    ppermute x3, waiting for transfers between devices, sum_strips(): lax.ppermute(sent, 'freq', [(i, (i + shift) % count) for i in range(count)])  12.3 us
    pallas_call x2, Pallas kernels, first(): pl.pallas_call(partial(first_kernel, sign), grid=(rows // step,), in_spec...  11.5 us
    reduce_scatter x1, waiting for transfers between devices, body(): piece = lax.psum_scatter(turned, 'freq', scatter_dimension=0, tiled=True)  11.3 us
    reduce_scatter x1, waiting for transfers between devices, body(): lax.psum_scatter(owned(1), 'freq', scatter_dimension=0, tiled=True)  10.7 us
    sin x2, other arithmetic, turning(): return (jnp.cos(theta), jnp.sin(theta))  10.2 us
  transfers between devices with their start and end apart: 14, of which 11 were waited for; matrix products, arithmetic and copies ran while one was open for 15% of the time, Pallas kernels for 19%

profile of v4, /device:TPU:2, one launch (start us, length us, event | category | flops | bytes accessed | tf_op | source)
XLA Modules:
  0.0 226.7 jit_solution(477998584570693566)
XLA Ops:
  9.8 2.5 %select_bitcast_fusion = (f32[256,1024]{1,0:T(8,128)}, f32[1,256,1024]{2,1,0:T(8,128)S(1)}) fusion(f32[1,256,1024]{2,1,0:T(8,128)} %param.7, pred[]{:T(512)S(6)} %eq.13, pred[]{:T(512)S(6)} %eq.12), kind=kLoop, calls=%fused_computation.31 | loop fusion | flops 524288 | bytes 3145730 | tf_op jit(solution)/shard_map/jit(_where)/select_n | solution.py:218
  14.0 3.5 %all-to-all-start = ((f32[4,256,256]{2,1,0:T(8,128)}), f32[4,256,256]{2,1,0:T(8,128)S(1)}, u32[]{:S(2)}, u32[]{:S(2)}) async-start(f32[4,256,256]{2,1,0:T(8,128)} %bitcast.26), calls=%async_computation | async-start | bytes 2097152 | tf_op jit(solution)/shard_map/all_to_all | solution.py:189
  18.3 4.3 %multiply_subtract_fusion = (f32[4,256,256]{2,1,0:T(8,128)S(1)}, f32[4,256,256]{2,1,0:T(8,128)S(1)}, f32[4,256,256]{2,1,0:T(8,128)S(1)}, f32[4,256,256]{2,1,0:T(8,128)S(1)}, f32[4,256,256]{2,1,0:T(8,128)S(1)}) fusion(f32[4,256]{1,0:T(4,128)S(1)} %get-tuple-element.65, f32[4,256]{1,0:T(4,128)S(1)} %get-tuple-element.64, s32[4,256]{1,0:T(4,128)S(1)} %iota_add_fusion), kind=kLoop, calls=%fused_computation.28 | loop fusion | flops 5505024 | bytes 5255168 | tf_op jit(solution)/shard_map/sub | solution.py:39
  22.7 3.7 %fusion.2 = f32[4,256,512]{2,1,0:T(8,128)S(1)} fusion(f32[4,256,256]{2,1,0:T(8,128)S(1)} %get-tuple-element.63, f32[4,256,256]{2,1,0:T(8,128)S(1)} %get-tuple-element.62, f32[4,256,256]{2,1,0:T(8,128)S(1)} %get-tuple-element.61, f32[4,256,256]{2,1,0:T(8,128)S(1)} %get-tuple-element.60, f32[4,256,256]{2,1,0:T(8,128)S(1)} %get-tuple-element.59), kind=kOutput, calls=%fused_computation.6 | convolution fusion | flops 3224895488 | bytes 7340032 | tf_op jit(solution)/shard_map/kbm,kcm->kbc/dot_general | solution.py:43
  28.0 2.1 all-to-all-done
  30.1 10.7 %reduce-scatter.4.cloned.1.call-done = f32[64,1024]{1,0:T(8,128)} async-done(((f32[256,1024]{1,0:T(8,128)}), f32[64,1024]{1,0:T(8,128)}) %reduce-scatter.4.cloned.1.call-update) | async-done | bytes 262160 | tf_op jit(solution)/shard_map/reduce_scatter | solution.py:221
  40.9 3.9 %reduce-precision_convert_fusion.1.high_ref = bf16[4,512,512]{2,1,0:T(8,128)(2,1)} fusion(f32[1,256,256]{2,1,0:T(8,128)S(1)} %get-tuple-element.46, f32[1,256,256]{2,1,0:T(8,128)} %get-tuple-element.47, f32[1,256,256]{2,1,0:T(8,128)} %get-tuple-element.48, f32[1,256,256]{2,1,0:T(8,128)} %get-tuple-element.49, f32[4,256,256]{2,1,0:T(8,128)S(1)} %maximum_multiply_fusion, ...), kind=kLoop, calls=%fused_computation.3 | loop fusion | flops 14680064 | bytes 5242880 | tf_op jit(solution)/shard_map/convert_element_type | solution.py:21
  44.8 3.1 %fusion.low_ref = bf16[4,512,512]{2,1,0:T(8,128)(2,1)} fusion(f32[1,256,256]{2,1,0:T(8,128)S(1)} %get-tuple-element.46, f32[1,256,256]{2,1,0:T(8,128)S(1)} %copy-done.5, f32[1,256,256]{2,1,0:T(8,128)S(1)} %copy-done.6, f32[1,256,256]{2,1,0:T(8,128)S(1)} %copy-done.7, f32[4,256,256]{2,1,0:T(8,128)S(1)} %maximum_multiply_fusion, ...), kind=kLoop, calls=%fused_computation.4 | loop fusion | flops 15728640 | bytes 5242880 | tf_op jit(solution)/shard_map/convert_element_type | solution.py:21
  48.0 5.7 %shard_map.77 = f32[4,2,256,256]{3,2,1,0:T(8,128)} custom-call(f32[2,1,256,1024]{3,2,1,0:T(8,128)} %field_ref.1, bf16[4,512,512]{2,1,0:T(8,128)(2,1)} %reduce-precision_convert_fusion.1.high_ref, bf16[4,512,512]{2,1,0:T(8,128)(2,1)} %fusion.low_ref), custom_call_target="tpu_custom_call" | custom-call | tf_op jit(solution)/shard_map/pallas_call | solution.py:252
  53.6 4.1 %all-to-all-start.2 = ((f32[4,2,256,256]{3,2,1,0:T(8,128)}), f32[4,2,256,256]{3,2,1,0:T(8,128)S(1)}, u32[]{:S(2)}, u32[]{:S(2)}) async-start(f32[4,2,256,256]{3,2,1,0:T(8,128)} %shard_map.77), calls=%async_computation.4 | async-start | bytes 4194304 | tf_op jit(solution)/shard_map/all_to_all | solution.py:189
  57.7 11.3 %reduce-scatter.6.cloned.1.call-done = f32[1,256,256]{2,1,0:T(8,128)} async-done(((f32[4,256,256]{2,1,0:T(8,128)}), f32[1,256,256]{2,1,0:T(8,128)}) %reduce-scatter.6.cloned.1.call-update) | async-done | bytes 262160 | tf_op jit(solution)/shard_map/reduce_scatter | solution.py:224
  69.1 5.8 %shard_map.76 = f32[4,2,256,256]{3,2,1,0:T(8,128)} custom-call(f32[2,1,256,1024]{3,2,1,0:T(8,128)} %field_ref, bf16[4,512,512]{2,1,0:T(8,128)(2,1)} %reduce-precision_convert_fusion.1.high_ref, bf16[4,512,512]{2,1,0:T(8,128)(2,1)} %fusion.low_ref), custom_call_target="tpu_custom_call" | custom-call | tf_op jit(solution)/shard_map/pallas_call | solution.py:252
  74.9 6.9 %all-to-all-done.2.field_ref = f32[4,2,256,256]{3,2,1,0:T(8,128)S(1)} async-done(((f32[4,2,256,256]{3,2,1,0:T(8,128)}), f32[4,2,256,256]{3,2,1,0:T(8,128)S(1)}, u32[]{:S(2)}, u32[]{:S(2)}) %all-to-all-start.2) | async-done | bytes 2097184 | tf_op jit(solution)/shard_map/all_to_all | solution.py:189
  83.1 5.2 %all-to-all-start.1 = ((f32[4,2,256,256]{3,2,1,0:T(8,128)}), f32[4,2,256,256]{3,2,1,0:T(8,128)S(1)}, u32[]{:S(2)}, u32[]{:S(2)}) async-start(f32[4,2,256,256]{3,2,1,0:T(8,128)} %shard_map.76), calls=%async_computation.3 | async-start | bytes 4194304 | tf_op jit(solution)/shard_map/all_to_all | solution.py:189
  88.3 1.8 broadcast_multiply_fusion
  90.2 2.4 %fusion.1 = (bf16[4,512,512]{2,1,0:T(8,128)(2,1)}, bf16[4,512,512]{2,1,0:T(8,128)(2,1)}) fusion(f32[4,256,256]{2,1,0:T(8,128)S(1)} %get-tuple-element.41, f32[4,256,256]{2,1,0:T(8,128)S(1)} %get-tuple-element.40, f32[4,256,256]{2,1,0:T(8,128)S(1)} %get-tuple-element.39), kind=kLoop, calls=%fused_computation.5 | loop fusion | flops 7340032 | bytes 7340032 | tf_op jit(solution)/shard_map/convert_element_type | solution.py:21
  92.5 4.7 %all-gather.3.cloned.1.call-done = f32[4,256,256]{2,1,0:T(8,128)} async-done(((f32[1,256,256]{2,1,0:T(8,128)}), f32[4,256,256]{2,1,0:T(8,128)}) %all-gather.3.cloned.1.call-update) | async-done | bytes 1048592 | tf_op jit(solution)/shard_map/all_gather | solution.py:226
  97.3 5.7 %multiply_sine_fusion.1 = (f32[4,256,256]{2,1,0:T(8,128)}, f32[4,256,256]{2,1,0:T(8,128)}) fusion(f32[4,256,256]{2,1,0:T(8,128)} %all-gather.3.cloned.1.call-done, f32[]{:T(128)} %bitcast.4), kind=kLoop, calls=%fused_computation.35 | loop fusion | flops 262144 | bytes 3145732 | tf_op jit(solution)/shard_map/sin | solution.py:215
  103.0 9.2 %shard_map.78 = (f32[4,2,256,256]{3,2,1,0:T(8,128)}, f32[4,2,256,256]{3,2,1,0:T(8,128)}) custom-call(f32[4,256,256]{2,1,0:T(8,128)} %get-tuple-element.56.cos_ref, f32[4,256,256]{2,1,0:T(8,128)} %get-tuple-element.55.sin_ref, f32[4,2,256,256]{3,2,1,0:T(8,128)} %copy-done.3, bf16[4,512,512]{2,1,0:T(8,128)(2,1)} %get-tuple-element.38.high_ref, ...), custom_call_target="tpu_custom_call" | custom-call | tf_op jit(solution)/shard_map/pallas_call | solution.py:283
  113.7 5.2 %all-to-all-start.3 = ((f32[4,2,256,256]{3,2,1,0:T(8,128)}), f32[4,2,256,256]{3,2,1,0:T(8,128)S(1)}, u32[]{:S(2)}, u32[]{:S(2)}) async-start(f32[4,2,256,256]{3,2,1,0:T(8,128)} %get-tuple-element.32), calls=%async_computation.5 | async-start | bytes 4194304 | tf_op jit(solution)/shard_map/all_to_all | solution.py:189
  118.9 9.8 %shard_map.79 = (f32[4,2,256,256]{3,2,1,0:T(8,128)}, f32[4,256,256]{2,1,0:T(8,128)}) custom-call(f32[4,256,256]{2,1,0:T(8,128)} %get-tuple-element.56.cos_ref, f32[4,256,256]{2,1,0:T(8,128)} %get-tuple-element.55.sin_ref, f32[4,2,256,256]{3,2,1,0:T(8,128)} %copy-done.1, bf16[4,512,512]{2,1,0:T(8,128)(2,1)} %get-tuple-element.38.high_ref, ...), custom_call_target="tpu_custom_call" | custom-call | tf_op jit(solution)/shard_map/pallas_call | solution.py:292
  128.8 14.2 %all-to-all-done.3.field_ref = f32[4,2,256,256]{3,2,1,0:T(8,128)S(1)} async-done(((f32[4,2,256,256]{3,2,1,0:T(8,128)}), f32[4,2,256,256]{3,2,1,0:T(8,128)S(1)}, u32[]{:S(2)}, u32[]{:S(2)}) %all-to-all-start.3) | async-done | bytes 2097184 | tf_op jit(solution)/shard_map/all_to_all | solution.py:189
  143.0 6.1 %all-to-all-start.4 = ((f32[4,2,256,256]{3,2,1,0:T(8,128)}), f32[4,2,256,256]{3,2,1,0:T(8,128)}, u32[]{:S(2)}, u32[]{:S(2)}) async-start(f32[4,2,256,256]{3,2,1,0:T(8,128)} %get-tuple-element.33), calls=%async_computation.6 | async-start | bytes 4194304 | tf_op jit(solution)/shard_map/all_to_all | solution.py:189
  149.1 4.5 %multiply_sine_fusion = (f32[256,1024]{1,0:T(8,128)}, f32[256,1024]{1,0:T(8,128)}) fusion(f32[256,1024]{1,0:T(8,128)S(1)} %copy-done.8, f32[]{:T(128)} %bitcast.4), kind=kLoop, calls=%fused_computation.33 | loop fusion | flops 262144 | bytes 3145732 | tf_op jit(solution)/shard_map/sin | solution.py:215
  153.6 6.2 %shard_map.80.source_ref = f32[2,1,256,1024]{3,2,1,0:T(8,128)} custom-call(f32[256,1024]{1,0:T(8,128)} %get-tuple-element.54.cos_ref, f32[256,1024]{1,0:T(8,128)} %get-tuple-element.53.sin_ref, f32[4,2,256,256]{3,2,1,0:T(8,128)} %copy-done, bf16[4,512,512]{2,1,0:T(8,128)(2,1)} %reduce-precision_convert_fusion.1.high_ref, bf16[4,512,512]{2,1,0:T(8,128)(2,1)} %fusion.low_ref), custom_call_target="tpu_custom_call" | custom-call | tf_op jit(solution)/shard_map/pallas_call | solution.py:317
  159.8 13.4 %all-to-all-done.4.field_ref = f32[4,2,256,256]{3,2,1,0:T(8,128)} async-done(((f32[4,2,256,256]{3,2,1,0:T(8,128)}), f32[4,2,256,256]{3,2,1,0:T(8,128)}, u32[]{:S(2)}, u32[]{:S(2)}) %all-to-all-start.4) | async-done | bytes 2097184 | tf_op jit(solution)/shard_map/all_to_all | solution.py:189
  173.2 6.9 %shard_map.81 = (f32[2,1,256,1024]{3,2,1,0:T(8,128)}, f32[4,256,256]{2,1,0:T(8,128)}) custom-call(f32[256,1024]{1,0:T(8,128)} %get-tuple-element.54.cos_ref, f32[256,1024]{1,0:T(8,128)} %get-tuple-element.53.sin_ref, f32[4,2,256,256]{3,2,1,0:T(8,128)} %all-to-all-done.4.field_ref, bf16[4,512,512]{2,1,0:T(8,128)(2,1)} %reduce-precision_convert_fusion.1.high_ref, ...), custom_call_target="tpu_custom_call" | custom-call | tf_op jit(solution)/shard_map/pallas_call | solution.py:325
  182.9 2.5 %collective-permute-start.3 = (f32[256,256]{1,0:T(8,128)S(1)}, f32[256,256]{1,0:T(8,128)S(1)}, u32[]{:S(2)}, u32[]{:S(2)}) collective-permute-start(f32[256,256]{1,0:T(8,128)S(1)} %get-tuple-element.51), channel_id=1, source_target_pairs={{0,3},{1,0},{2,1},{3,2},{4,7},{5,4},{6,5},{7,6},{8,11},{9,8},{10,9... | collective-permute-start | bytes 786440 | tf_op jit(solution)/shard_map/ppermute | solution.py:198
  185.4 4.7 %collective-permute-start = (f32[256,256]{1,0:T(8,128)}, f32[256,256]{1,0:T(8,128)S(1)}, u32[]{:S(2)}, u32[]{:S(2)}) collective-permute-start(f32[256,256]{1,0:T(8,128)} %reduce-scatter.8.cloned.1.call-done), channel_id=1, source_target_pairs={{0,0},{1,4},{2,8},{3,12},{4,1},{5,5},{6,9},{7,13},{8,2},{9,6},{10,... | collective-permute-start | bytes 786440 | tf_op jit(solution)/shard_map/ppermute | solution.py:312
  190.1 2.2 collective-permute-done.1
  192.4 10.1 %collective-permute-done.2 = f32[256,256]{1,0:T(8,128)S(1)} collective-permute-done((f32[256,256]{1,0:T(8,128)S(1)}, f32[256,256]{1,0:T(8,128)S(1)}, u32[]{:S(2)}, u32[]{:S(2)}) %collective-permute-start.2) | collective-permute-done | bytes 262176 | tf_op jit(solution)/shard_map/ppermute | solution.py:198
  203.5 15.9 %collective-permute-done = f32[256,256]{1,0:T(8,128)S(1)} collective-permute-done((f32[256,256]{1,0:T(8,128)}, f32[256,256]{1,0:T(8,128)S(1)}, u32[]{:S(2)}, u32[]{:S(2)}) %collective-permute-start) | collective-permute-done | bytes 262176 | tf_op jit(solution)/shard_map/ppermute | solution.py:312
  (45 shorter events, 12.4 us)
Async XLA Ops:
  7.2 33.7 %reduce-scatter.4.cloned.1.call-start = ((), (), s32[]{:S(2)}) async-start(), calls=%async_computation.8 | async-start | bytes 1310720 | tf_op jit(solution)/shard_map/reduce_scatter | solution.py:221
  14.0 16.1 %all-to-all-start = ((f32[4,256,256]{2,1,0:T(8,128)}), f32[4,256,256]{2,1,0:T(8,128)S(1)}, u32[]{:S(2)}, u32[]{:S(2)}) async-start(f32[4,256,256]{2,1,0:T(8,128)} %bitcast.26), calls=%async_computation | async-start | bytes 2097152 | tf_op jit(solution)/shard_map/all_to_all | solution.py:189
  17.5 51.5 %reduce-scatter.6.cloned.1.call-start = ((), (), s32[]{:S(2)}) async-start(), calls=%async_computation.9 | async-start | bytes 1310720 | tf_op jit(solution)/shard_map/reduce_scatter | solution.py:224
  26.4 1.6 copy-start.2
  30.1 10.7 %copy-start.4 = (f32[4,256,256]{2,1,0:T(8,128)}, f32[4,256,256]{2,1,0:T(8,128)S(1)}, u32[]{:S(2)}) copy-start(f32[4,256,256]{2,1,0:T(8,128)S(1)} %all-to-all-done) | copy-start | bytes 3145732
  40.9 3.9 %copy-start.5 = (f32[1,256,256]{2,1,0:T(8,128)S(1)}, f32[1,256,256]{2,1,0:T(8,128)}, u32[]{:S(2)}) copy-start(f32[1,256,256]{2,1,0:T(8,128)} %get-tuple-element.47) | copy-start | bytes 786436
  40.9 3.9 %copy-start.6 = (f32[1,256,256]{2,1,0:T(8,128)S(1)}, f32[1,256,256]{2,1,0:T(8,128)}, u32[]{:S(2)}) copy-start(f32[1,256,256]{2,1,0:T(8,128)} %get-tuple-element.48) | copy-start | bytes 786436
  40.9 3.9 %copy-start.7 = (f32[1,256,256]{2,1,0:T(8,128)S(1)}, f32[1,256,256]{2,1,0:T(8,128)}, u32[]{:S(2)}) copy-start(f32[1,256,256]{2,1,0:T(8,128)} %get-tuple-element.49) | copy-start | bytes 786436
  53.6 28.1 %all-to-all-start.2 = ((f32[4,2,256,256]{3,2,1,0:T(8,128)}), f32[4,2,256,256]{3,2,1,0:T(8,128)S(1)}, u32[]{:S(2)}, u32[]{:S(2)}) async-start(f32[4,2,256,256]{3,2,1,0:T(8,128)} %shard_map.77), calls=%async_computation.4 | async-start | bytes 4194304 | tf_op jit(solution)/shard_map/all_to_all | solution.py:189
  57.7 39.5 %all-gather.3.cloned.1.call-start = ((), (), s32[]{:S(2)}) async-start(), calls=%async_computation.10 | async-start | bytes 1310720 | tf_op jit(solution)/shard_map/all_gather | solution.py:226
  81.8 1.3 copy-start.3
  83.1 29.3 %all-to-all-start.1 = ((f32[4,2,256,256]{3,2,1,0:T(8,128)}), f32[4,2,256,256]{3,2,1,0:T(8,128)S(1)}, u32[]{:S(2)}, u32[]{:S(2)}) async-start(f32[4,2,256,256]{3,2,1,0:T(8,128)} %shard_map.76), calls=%async_computation.3 | async-start | bytes 4194304 | tf_op jit(solution)/shard_map/all_to_all | solution.py:189
  88.3 40.4 %all-gather.5.cloned.1.call-start = ((), (), s32[]{:S(2)}) async-start(), calls=%async_computation.11 | async-start | bytes 1310720 | tf_op jit(solution)/shard_map/all_gather | solution.py:228
  112.4 1.3 copy-start.1
  113.7 29.3 %all-to-all-start.3 = ((f32[4,2,256,256]{3,2,1,0:T(8,128)}), f32[4,2,256,256]{3,2,1,0:T(8,128)S(1)}, u32[]{:S(2)}, u32[]{:S(2)}) async-start(f32[4,2,256,256]{3,2,1,0:T(8,128)} %get-tuple-element.32), calls=%async_computation.5 | async-start | bytes 4194304 | tf_op jit(solution)/shard_map/all_to_all | solution.py:189
  118.9 66.5 %reduce-scatter.8.cloned.1.call-start = ((), (), s32[]{:S(2)}) async-start(), calls=%async_computation.12 | async-start | bytes 1310720 | tf_op jit(solution)/shard_map/reduce_scatter | solution.py:306
  128.8 20.3 %copy-start.8 = (f32[256,1024]{1,0:T(8,128)S(1)}, f32[256,1024]{1,0:T(8,128)}, u32[]{:S(2)}) copy-start(f32[256,1024]{1,0:T(8,128)} %all-gather.5.cloned.1.call-done) | copy-start | bytes 3145732
  143.0 6.1 %copy-start = (f32[4,2,256,256]{3,2,1,0:T(8,128)}, f32[4,2,256,256]{3,2,1,0:T(8,128)S(1)}, u32[]{:S(2)}) copy-start(f32[4,2,256,256]{3,2,1,0:T(8,128)S(1)} %all-to-all-done.3.field_ref) | copy-start | bytes 6291460
  143.0 30.2 %all-to-all-start.4 = ((f32[4,2,256,256]{3,2,1,0:T(8,128)}), f32[4,2,256,256]{3,2,1,0:T(8,128)}, u32[]{:S(2)}, u32[]{:S(2)}) async-start(f32[4,2,256,256]{3,2,1,0:T(8,128)} %get-tuple-element.33), calls=%async_computation.6 | async-start | bytes 4194304 | tf_op jit(solution)/shard_map/all_to_all | solution.py:189
  181.2 11.2 %collective-permute-start.1 = (f32[256,256]{1,0:T(8,128)S(1)}, f32[256,256]{1,0:T(8,128)S(1)}, u32[]{:S(2)}, u32[]{:S(2)}) collective-permute-start(f32[256,256]{1,0:T(8,128)S(1)} %get-tuple-element.50), channel_id=1, source_target_pairs={{0,1},{1,2},{2,3},{3,0},{4,5},{5,6},{6,7},{7,4},{8,9},{9,10},{10,1... | collective-permute-start | bytes 786440 | tf_op jit(solution)/shard_map/ppermute | solution.py:198
  181.5 21.0 %collective-permute-start.2 = (f32[256,256]{1,0:T(8,128)S(1)}, f32[256,256]{1,0:T(8,128)S(1)}, u32[]{:S(2)}, u32[]{:S(2)}) collective-permute-start(f32[256,256]{1,0:T(8,128)S(1)} %get-tuple-element.52), channel_id=1, source_target_pairs={{0,2},{1,3},{2,0},{3,1},{4,6},{5,7},{6,4},{7,5},{8,10},{9,11},{10,... | collective-permute-start | bytes 786440 | tf_op jit(solution)/shard_map/ppermute | solution.py:198
  182.9 19.6 %collective-permute-start.3 = (f32[256,256]{1,0:T(8,128)S(1)}, f32[256,256]{1,0:T(8,128)S(1)}, u32[]{:S(2)}, u32[]{:S(2)}) collective-permute-start(f32[256,256]{1,0:T(8,128)S(1)} %get-tuple-element.51), channel_id=1, source_target_pairs={{0,3},{1,0},{2,1},{3,2},{4,7},{5,4},{6,5},{7,6},{8,11},{9,8},{10,9... | collective-permute-start | bytes 786440 | tf_op jit(solution)/shard_map/ppermute | solution.py:198
  185.4 34.0 %collective-permute-start = (f32[256,256]{1,0:T(8,128)}, f32[256,256]{1,0:T(8,128)S(1)}, u32[]{:S(2)}, u32[]{:S(2)}) collective-permute-start(f32[256,256]{1,0:T(8,128)} %reduce-scatter.8.cloned.1.call-done), channel_id=1, source_target_pairs={{0,0},{1,4},{2,8},{3,12},{4,1},{5,5},{6,9},{7,13},{8,2},{9,6},{10,... | collective-permute-start | bytes 786440 | tf_op jit(solution)/shard_map/ppermute | solution.py:312
Sparse Core Ops, SparseCore 0:
  12.4 28.3 reduce-scatter.3
  43.2 25.7 reduce-scatter.5
  70.6 26.5 all-gather.2
  98.7 27.4 all-gather.4
  128.9 25.9 reduce-scatter.7

commit v5 on v4

--- a/solution.py
+++ b/solution.py
@@ -220,7 +220,6 @@
     turned = swap(jnp.moveaxis(owned(0).reshape(rows, row_count, cols), 1, 0))
     piece_last = lax.psum_scatter(owned(1), "freq", scatter_dimension=0, tiled=True)
     source_field, turned = lax.optimization_barrier((source_field, turned))
-    turned, piece_last = lax.optimization_barrier((turned, piece_last))
     piece = lax.psum_scatter(turned, "freq", scatter_dimension=0, tiled=True)
     receiver_field, piece = lax.optimization_barrier((receiver_field, piece))
     slab_first = lax.all_gather(piece, "freq", axis=0, tiled=True)

time: 228 us -> 246 us (1.079)
  blocking collectives: 0 us -> 16 us
  waiting for transfers between devices: 91.8 us -> 98.5 us
  starting transfers between devices: 33.2 us -> 29.7 us
    all_gather x1, waiting for transfers between devices: 4.75 us -> 22.9 us  [body(): slab_first = lax.all_gather(piece, 'freq', axis=0, tiled=True)]
    all_to_all x0 -> x1, blocking collectives: none -> 16 us  [swap(): lax.all_to_all(blocks, 'row', split_axis=0, concat_axis=0, tiled=True)]
    reduce_scatter x1, waiting for transfers between devices: 10.7 us -> 0.01 us  [body(): lax.psum_scatter(owned(1), 'freq', scatter_dimension=0, tiled=True)]
    reduce_scatter x1, waiting for transfers between devices: 11.3 us -> 1.3 us  [body(): piece = lax.psum_scatter(turned, 'freq', scatter_dimension=0, tiled=True)]
    all_to_all x5 -> x4, waiting for transfers between devices: 36.6 us -> 44.5 us  [swap(): lax.all_to_all(blocks, 'row', split_axis=0, concat_axis=0, tiled=True)]
    all_to_all x5 -> x4, starting transfers between devices: 24.2 us -> 20.7 us  [swap(): lax.all_to_all(blocks, 'row', split_axis=0, concat_axis=0, tiled=True)]
    unnamed x18 -> x10, local copies, waits for them, and re-layouts: 3.04 us -> 5.07 us
  transfers between devices with their start and end apart: 14 -> 13, of which waited for: 11 -> 8; matrix products, arithmetic and copies ran while one was open for 15% -> 13% of each run, Pallas kernels for 19% -> 18%
where the time goes in v5:
time: 246 us; the launch traced here: 245 us
  waiting for transfers between devices  98.5 us (40%)
  Pallas kernels  43.6 us (18%)
  starting transfers between devices  29.7 us (12%)
  other arithmetic  29.2 us (12%)
  blocking collectives  16 us (7%)
  between operations  15.9 us (6%)
  local copies, waits for them, and re-layouts  8.43 us (3%)
  matrix products  3.71 us (2%)
    all_to_all x4, waiting for transfers between devices, swap(): lax.all_to_all(blocks, 'row', split_axis=0, concat_axis=0, tiled=True)  44.5 us
    all_gather x1, waiting for transfers between devices, body(): slab_first = lax.all_gather(piece, 'freq', axis=0, tiled=True)  22.9 us
    all_to_all x4, starting transfers between devices, swap(): lax.all_to_all(blocks, 'row', split_axis=0, concat_axis=0, tiled=True)  20.7 us
    ppermute x1, waiting for transfers between devices, body(): image_first = lax.ppermute(part, ('row', 'freq'), pairs)  16.8 us
    all_to_all x1, blocking collectives, swap(): lax.all_to_all(blocks, 'row', split_axis=0, concat_axis=0, tiled=True)  16 us
    ppermute x3, waiting for transfers between devices, sum_strips(): lax.ppermute(sent, 'freq', [(i, (i + shift) % count) for i in range(count)])  12.3 us
    pallas_call x2, Pallas kernels, first(): pl.pallas_call(partial(first_kernel, sign), grid=(rows // step,), in_spec...  11.4 us
    sin x2, other arithmetic, turning(): return (jnp.cos(theta), jnp.sin(theta))  10.2 us
  transfers between devices with their start and end apart: 13, of which 8 were waited for; matrix products, arithmetic and copies ran while one was open for 13% of the time, Pallas kernels for 18%

profile of v5, /device:TPU:2, one launch (start us, length us, event | category | flops | bytes accessed | tf_op | source)
XLA Modules:
  0.0 245.0 jit_solution(469321549130511808)
XLA Ops:
  9.8 2.5 %broadcast_select_fusion = (f32[1,256,1024]{2,1,0:T(8,128)S(1)}, f32[256,1024]{1,0:T(8,128)}) fusion(f32[1,256,1024]{2,1,0:T(8,128)} %param.7, pred[]{:T(512)S(6)} %eq.13, pred[]{:T(512)S(6)} %eq.12), kind=kLoop, calls=%fused_computation.42 | loop fusion | flops 524288 | bytes 3145730 | tf_op jit(solution)/shard_map/jit(_where)/select_n | solution.py:218
  13.0 16.0 %all_to_all.25 = f32[4,256,256]{2,1,0:T(8,128)} all-to-all(f32[4,256,256]{2,1,0:T(8,128)S(1)} %bitcast.27), channel_id=1, replica_groups=mesh['shot'=2,'row'=4,'freq'=4] {'row'}, dimensions={0} | all-to-all | bytes 2097152 | tf_op jit(solution)/shard_map/all_to_all | solution.py:189
  30.6 4.3 %multiply_subtract_fusion = (f32[4,256,256]{2,1,0:T(8,128)S(1)}, f32[4,256,256]{2,1,0:T(8,128)S(1)}, f32[4,256,256]{2,1,0:T(8,128)S(1)}, f32[4,256,256]{2,1,0:T(8,128)S(1)}, f32[4,256,256]{2,1,0:T(8,128)S(1)}) fusion(f32[4,256]{1,0:T(4,128)S(1)} %get-tuple-element.61, f32[4,256]{1,0:T(4,128)S(1)} %get-tuple-element.60, s32[4,256]{1,0:T(4,128)S(1)} %iota_add_fusion), kind=kLoop, calls=%fused_computation.28 | loop fusion | flops 5505024 | bytes 5255168 | tf_op jit(solution)/shard_map/sub | solution.py:39
  34.9 3.7 %fusion.2 = f32[4,256,512]{2,1,0:T(8,128)S(1)} fusion(f32[4,256,256]{2,1,0:T(8,128)S(1)} %get-tuple-element.59, f32[4,256,256]{2,1,0:T(8,128)S(1)} %get-tuple-element.58, f32[4,256,256]{2,1,0:T(8,128)S(1)} %get-tuple-element.57, f32[4,256,256]{2,1,0:T(8,128)S(1)} %get-tuple-element.56, f32[4,256,256]{2,1,0:T(8,128)S(1)} %get-tuple-element.55), kind=kOutput, calls=%fused_computation.6 | convolution fusion | flops 3224895488 | bytes 7340032 | tf_op jit(solution)/shard_map/kbm,kcm->kbc/dot_general | solution.py:43
  40.0 2.9 %reduce-precision_convert_fusion.1.high_ref = bf16[4,512,512]{2,1,0:T(8,128)(2,1)} fusion(f32[1,256,256]{2,1,0:T(8,128)S(1)} %get-tuple-element.42, f32[1,256,256]{2,1,0:T(8,128)S(1)} %get-tuple-element.43, f32[1,256,256]{2,1,0:T(8,128)S(1)} %get-tuple-element.44, f32[1,256,256]{2,1,0:T(8,128)S(1)} %get-tuple-element.45, ...), kind=kLoop, calls=%fused_computation.3 | loop fusion | flops 14680064 | bytes 5242880 | tf_op jit(solution)/shard_map/convert_element_type | solution.py:21
  43.0 3.1 %fusion.low_ref = bf16[4,512,512]{2,1,0:T(8,128)(2,1)} fusion(f32[1,256,256]{2,1,0:T(8,128)S(1)} %get-tuple-element.42, f32[1,256,256]{2,1,0:T(8,128)S(1)} %get-tuple-element.43, f32[1,256,256]{2,1,0:T(8,128)S(1)} %get-tuple-element.44, f32[1,256,256]{2,1,0:T(8,128)S(1)} %get-tuple-element.45, f32[4,256,256]{2,1,0:T(8,128)S(1)} %maximum_multiply_fusion, ...), kind=kLoop, calls=%fused_computation.4 | loop fusion | flops 15728640 | bytes 5242880 | tf_op jit(solution)/shard_map/convert_element_type | solution.py:21
  46.1 5.7 %shard_map.77 = f32[4,2,256,256]{3,2,1,0:T(8,128)} custom-call(f32[2,1,256,1024]{3,2,1,0:T(8,128)} %field_ref.1, bf16[4,512,512]{2,1,0:T(8,128)(2,1)} %reduce-precision_convert_fusion.1.high_ref, bf16[4,512,512]{2,1,0:T(8,128)(2,1)} %fusion.low_ref), custom_call_target="tpu_custom_call" | custom-call | tf_op jit(solution)/shard_map/pallas_call | solution.py:251
  51.7 5.3 %all-to-all-start.2 = ((f32[4,2,256,256]{3,2,1,0:T(8,128)}), f32[4,2,256,256]{3,2,1,0:T(8,128)S(1)}, u32[]{:S(2)}, u32[]{:S(2)}) async-start(f32[4,2,256,256]{3,2,1,0:T(8,128)} %shard_map.77), calls=%async_computation.4 | async-start | bytes 4194304 | tf_op jit(solution)/shard_map/all_to_all | solution.py:189
  58.3 5.8 %shard_map.76 = f32[4,2,256,256]{3,2,1,0:T(8,128)} custom-call(f32[2,1,256,1024]{3,2,1,0:T(8,128)} %field_ref, bf16[4,512,512]{2,1,0:T(8,128)(2,1)} %reduce-precision_convert_fusion.1.high_ref, bf16[4,512,512]{2,1,0:T(8,128)(2,1)} %fusion.low_ref), custom_call_target="tpu_custom_call" | custom-call | tf_op jit(solution)/shard_map/pallas_call | solution.py:251
  64.1 17.0 %all-to-all-done.2.field_ref = f32[4,2,256,256]{3,2,1,0:T(8,128)S(1)} async-done(((f32[4,2,256,256]{3,2,1,0:T(8,128)}), f32[4,2,256,256]{3,2,1,0:T(8,128)S(1)}, u32[]{:S(2)}, u32[]{:S(2)}) %all-to-all-start.2) | async-done | bytes 2097184 | tf_op jit(solution)/shard_map/all_to_all | solution.py:189
  81.0 1.3 copy-done.3
  82.3 5.2 %all-to-all-start.1 = ((f32[4,2,256,256]{3,2,1,0:T(8,128)}), f32[4,2,256,256]{3,2,1,0:T(8,128)S(1)}, u32[]{:S(2)}, u32[]{:S(2)}) async-start(f32[4,2,256,256]{3,2,1,0:T(8,128)} %shard_map.76), calls=%async_computation.3 | async-start | bytes 4194304 | tf_op jit(solution)/shard_map/all_to_all | solution.py:189
  87.6 1.8 broadcast_multiply_fusion
  89.4 2.4 fusion.1
  91.8 22.9 %all-gather.3.cloned.1.call-done = f32[4,256,256]{2,1,0:T(8,128)} async-done(((f32[1,256,256]{2,1,0:T(8,128)}), f32[4,256,256]{2,1,0:T(8,128)}) %all-gather.3.cloned.1.call-update) | async-done | bytes 1048592 | tf_op jit(solution)/shard_map/all_gather | solution.py:225
  114.7 5.7 %multiply_sine_fusion.1 = (f32[4,256,256]{2,1,0:T(8,128)}, f32[4,256,256]{2,1,0:T(8,128)}) fusion(f32[4,256,256]{2,1,0:T(8,128)} %all-gather.3.cloned.1.call-done, f32[]{:T(128)} %bitcast.4), kind=kLoop, calls=%fused_computation.35 | loop fusion | flops 262144 | bytes 3145732 | tf_op jit(solution)/shard_map/sin | solution.py:215
  120.4 9.3 %shard_map.78 = (f32[4,2,256,256]{3,2,1,0:T(8,128)}, f32[4,2,256,256]{3,2,1,0:T(8,128)}) custom-call(f32[4,256,256]{2,1,0:T(8,128)} %get-tuple-element.52.cos_ref, f32[4,256,256]{2,1,0:T(8,128)} %get-tuple-element.51.sin_ref, f32[4,2,256,256]{3,2,1,0:T(8,128)} %copy-done.3, bf16[4,512,512]{2,1,0:T(8,128)(2,1)} %get-tuple-element.34.high_ref, ...), custom_call_target="tpu_custom_call" | custom-call | tf_op jit(solution)/shard_map/pallas_call | solution.py:282
  131.0 4.2 %all-to-all-start.3 = ((f32[4,2,256,256]{3,2,1,0:T(8,128)}), f32[4,2,256,256]{3,2,1,0:T(8,128)S(1)}, u32[]{:S(2)}, u32[]{:S(2)}) async-start(f32[4,2,256,256]{3,2,1,0:T(8,128)} %get-tuple-element.28), calls=%async_computation.5 | async-start | bytes 4194304 | tf_op jit(solution)/shard_map/all_to_all | solution.py:189
  135.1 9.9 %shard_map.79 = (f32[4,2,256,256]{3,2,1,0:T(8,128)}, f32[4,256,256]{2,1,0:T(8,128)}) custom-call(f32[4,256,256]{2,1,0:T(8,128)} %get-tuple-element.52.cos_ref, f32[4,256,256]{2,1,0:T(8,128)} %get-tuple-element.51.sin_ref, f32[4,2,256,256]{3,2,1,0:T(8,128)} %copy-done.1, bf16[4,512,512]{2,1,0:T(8,128)(2,1)} %get-tuple-element.34.high_ref, ...), custom_call_target="tpu_custom_call" | custom-call | tf_op jit(solution)/shard_map/pallas_call | solution.py:291
  145.0 14.1 %all-to-all-done.3.field_ref = f32[4,2,256,256]{3,2,1,0:T(8,128)S(1)} async-done(((f32[4,2,256,256]{3,2,1,0:T(8,128)}), f32[4,2,256,256]{3,2,1,0:T(8,128)S(1)}, u32[]{:S(2)}, u32[]{:S(2)}) %all-to-all-start.3) | async-done | bytes 2097184 | tf_op jit(solution)/shard_map/all_to_all | solution.py:189
  159.2 1.3 copy-done
  160.5 6.1 %all-to-all-start.4 = ((f32[4,2,256,256]{3,2,1,0:T(8,128)}), f32[4,2,256,256]{3,2,1,0:T(8,128)}, u32[]{:S(2)}, u32[]{:S(2)}) async-start(f32[4,2,256,256]{3,2,1,0:T(8,128)} %get-tuple-element.29), calls=%async_computation.6 | async-start | bytes 4194304 | tf_op jit(solution)/shard_map/all_to_all | solution.py:189
  166.6 4.5 %multiply_sine_fusion = (f32[256,1024]{1,0:T(8,128)}, f32[256,1024]{1,0:T(8,128)}) fusion(f32[256,1024]{1,0:T(8,128)S(1)} %copy-done.4, f32[]{:T(128)} %bitcast.4), kind=kLoop, calls=%fused_computation.33 | loop fusion | flops 262144 | bytes 3145732 | tf_op jit(solution)/shard_map/sin | solution.py:215
  171.1 6.2 %shard_map.80.source_ref = f32[2,1,256,1024]{3,2,1,0:T(8,128)} custom-call(f32[256,1024]{1,0:T(8,128)} %get-tuple-element.50.cos_ref, f32[256,1024]{1,0:T(8,128)} %get-tuple-element.49.sin_ref, f32[4,2,256,256]{3,2,1,0:T(8,128)} %copy-done, bf16[4,512,512]{2,1,0:T(8,128)(2,1)} %reduce-precision_convert_fusion.1.high_ref, bf16[4,512,512]{2,1,0:T(8,128)(2,1)} %fusion.low_ref), custom_call_target="tpu_custom_call" | custom-call | tf_op jit(solution)/shard_map/pallas_call | solution.py:316
  177.3 13.4 %all-to-all-done.4.field_ref = f32[4,2,256,256]{3,2,1,0:T(8,128)} async-done(((f32[4,2,256,256]{3,2,1,0:T(8,128)}), f32[4,2,256,256]{3,2,1,0:T(8,128)}, u32[]{:S(2)}, u32[]{:S(2)}) %all-to-all-start.4) | async-done | bytes 2097184 | tf_op jit(solution)/shard_map/all_to_all | solution.py:189
  190.7 6.8 %shard_map.81 = (f32[2,1,256,1024]{3,2,1,0:T(8,128)}, f32[4,256,256]{2,1,0:T(8,128)}) custom-call(f32[256,1024]{1,0:T(8,128)} %get-tuple-element.50.cos_ref, f32[256,1024]{1,0:T(8,128)} %get-tuple-element.49.sin_ref, f32[4,2,256,256]{3,2,1,0:T(8,128)} %all-to-all-done.4.field_ref, bf16[4,512,512]{2,1,0:T(8,128)(2,1)} %reduce-precision_convert_fusion.1.high_ref, ...), custom_call_target="tpu_custom_call" | custom-call | tf_op jit(solution)/shard_map/pallas_call | solution.py:324
  198.7 1.5 collective-permute-start.1
  201.0 2.5 %collective-permute-start.3 = (f32[256,256]{1,0:T(8,128)S(1)}, f32[256,256]{1,0:T(8,128)S(1)}, u32[]{:S(2)}, u32[]{:S(2)}) collective-permute-start(f32[256,256]{1,0:T(8,128)S(1)} %get-tuple-element.47), channel_id=1, source_target_pairs={{0,3},{1,0},{2,1},{3,2},{4,7},{5,4},{6,5},{7,6},{8,11},{9,8},{10,9... | collective-permute-start | bytes 786440 | tf_op jit(solution)/shard_map/ppermute | solution.py:198
  203.5 4.1 %collective-permute-start = (f32[256,256]{1,0:T(8,128)}, f32[256,256]{1,0:T(8,128)S(1)}, u32[]{:S(2)}, u32[]{:S(2)}) collective-permute-start(f32[256,256]{1,0:T(8,128)} %reduce-scatter.8.cloned.1.call-done), channel_id=1, source_target_pairs={{0,0},{1,4},{2,8},{3,12},{4,1},{5,5},{6,9},{7,13},{8,2},{9,6},{10,... | collective-permute-start | bytes 786440 | tf_op jit(solution)/shard_map/ppermute | solution.py:311
  207.6 2.3 collective-permute-done.1
  209.9 10.0 %collective-permute-done.2 = f32[256,256]{1,0:T(8,128)S(1)} collective-permute-done((f32[256,256]{1,0:T(8,128)S(1)}, f32[256,256]{1,0:T(8,128)S(1)}, u32[]{:S(2)}, u32[]{:S(2)}) %collective-permute-start.2) | collective-permute-done | bytes 262176 | tf_op jit(solution)/shard_map/ppermute | solution.py:198
  220.9 16.8 %collective-permute-done = f32[256,256]{1,0:T(8,128)S(1)} collective-permute-done((f32[256,256]{1,0:T(8,128)}, f32[256,256]{1,0:T(8,128)S(1)}, u32[]{:S(2)}, u32[]{:S(2)}) %collective-permute-start) | collective-permute-done | bytes 262176 | tf_op jit(solution)/shard_map/ppermute | solution.py:311
  (36 shorter events, 10.8 us)
Async XLA Ops:
  7.2 51.1 %reduce-scatter.6.cloned.1.call-start = ((), (), s32[]{:S(2)}) async-start(), calls=%async_computation.9 | async-start | bytes 1310720 | tf_op jit(solution)/shard_map/reduce_scatter | solution.py:223
  29.1 62.7 %reduce-scatter.4.cloned.1.call-start = ((), (), s32[]{:S(2)}) async-start(), calls=%async_computation.8 | async-start | bytes 1310720 | tf_op jit(solution)/shard_map/reduce_scatter | solution.py:221
  38.6 1.3 copy-start.2
  51.7 29.3 %all-to-all-start.2 = ((f32[4,2,256,256]{3,2,1,0:T(8,128)}), f32[4,2,256,256]{3,2,1,0:T(8,128)S(1)}, u32[]{:S(2)}, u32[]{:S(2)}) async-start(f32[4,2,256,256]{3,2,1,0:T(8,128)} %shard_map.77), calls=%async_computation.4 | async-start | bytes 4194304 | tf_op jit(solution)/shard_map/all_to_all | solution.py:189
  57.0 57.7 %all-gather.3.cloned.1.call-start = ((), (), s32[]{:S(2)}) async-start(), calls=%async_computation.10 | async-start | bytes 1310720 | tf_op jit(solution)/shard_map/all_gather | solution.py:225
  81.0 1.3 copy-start.3
  82.3 47.3 %all-to-all-start.1 = ((f32[4,2,256,256]{3,2,1,0:T(8,128)}), f32[4,2,256,256]{3,2,1,0:T(8,128)S(1)}, u32[]{:S(2)}, u32[]{:S(2)}) async-start(f32[4,2,256,256]{3,2,1,0:T(8,128)} %shard_map.76), calls=%async_computation.3 | async-start | bytes 4194304 | tf_op jit(solution)/shard_map/all_to_all | solution.py:189
  87.6 57.4 %all-gather.5.cloned.1.call-start = ((), (), s32[]{:S(2)}) async-start(), calls=%async_computation.11 | async-start | bytes 1310720 | tf_op jit(solution)/shard_map/all_gather | solution.py:227
  129.6 1.3 copy-start.1
  131.0 28.2 %all-to-all-start.3 = ((f32[4,2,256,256]{3,2,1,0:T(8,128)}), f32[4,2,256,256]{3,2,1,0:T(8,128)S(1)}, u32[]{:S(2)}, u32[]{:S(2)}) async-start(f32[4,2,256,256]{3,2,1,0:T(8,128)} %get-tuple-element.28), calls=%async_computation.5 | async-start | bytes 4194304 | tf_op jit(solution)/shard_map/all_to_all | solution.py:189
  135.1 68.4 %reduce-scatter.8.cloned.1.call-start = ((), (), s32[]{:S(2)}) async-start(), calls=%async_computation.12 | async-start | bytes 1310720 | tf_op jit(solution)/shard_map/reduce_scatter | solution.py:305
  145.0 21.6 %copy-start.4 = (f32[256,1024]{1,0:T(8,128)S(1)}, f32[256,1024]{1,0:T(8,128)}, u32[]{:S(2)}) copy-start(f32[256,1024]{1,0:T(8,128)} %all-gather.5.cloned.1.call-done) | copy-start | bytes 3145732
  159.2 1.3 copy-start
  160.5 30.2 %all-to-all-start.4 = ((f32[4,2,256,256]{3,2,1,0:T(8,128)}), f32[4,2,256,256]{3,2,1,0:T(8,128)}, u32[]{:S(2)}, u32[]{:S(2)}) async-start(f32[4,2,256,256]{3,2,1,0:T(8,128)} %get-tuple-element.29), calls=%async_computation.6 | async-start | bytes 4194304 | tf_op jit(solution)/shard_map/all_to_all | solution.py:189
  198.7 11.2 %collective-permute-start.1 = (f32[256,256]{1,0:T(8,128)S(1)}, f32[256,256]{1,0:T(8,128)S(1)}, u32[]{:S(2)}, u32[]{:S(2)}) collective-permute-start(f32[256,256]{1,0:T(8,128)S(1)} %get-tuple-element.46), channel_id=1, source_target_pairs={{0,1},{1,2},{2,3},{3,0},{4,5},{5,6},{6,7},{7,4},{8,9},{9,10},{10,1... | collective-permute-start | bytes 786440 | tf_op jit(solution)/shard_map/ppermute | solution.py:198
  200.2 19.7 %collective-permute-start.2 = (f32[256,256]{1,0:T(8,128)S(1)}, f32[256,256]{1,0:T(8,128)S(1)}, u32[]{:S(2)}, u32[]{:S(2)}) collective-permute-start(f32[256,256]{1,0:T(8,128)S(1)} %get-tuple-element.48), channel_id=1, source_target_pairs={{0,2},{1,3},{2,0},{3,1},{4,6},{5,7},{6,4},{7,5},{8,10},{9,11},{10,... | collective-permute-start | bytes 786440 | tf_op jit(solution)/shard_map/ppermute | solution.py:198
  201.0 18.9 %collective-permute-start.3 = (f32[256,256]{1,0:T(8,128)S(1)}, f32[256,256]{1,0:T(8,128)S(1)}, u32[]{:S(2)}, u32[]{:S(2)}) collective-permute-start(f32[256,256]{1,0:T(8,128)S(1)} %get-tuple-element.47), channel_id=1, source_target_pairs={{0,3},{1,0},{2,1},{3,2},{4,7},{5,4},{6,5},{7,6},{8,11},{9,8},{10,9... | collective-permute-start | bytes 786440 | tf_op jit(solution)/shard_map/ppermute | solution.py:198
  203.5 34.2 %collective-permute-start = (f32[256,256]{1,0:T(8,128)}, f32[256,256]{1,0:T(8,128)S(1)}, u32[]{:S(2)}, u32[]{:S(2)}) collective-permute-start(f32[256,256]{1,0:T(8,128)} %reduce-scatter.8.cloned.1.call-done), channel_id=1, source_target_pairs={{0,0},{1,4},{2,8},{3,12},{4,1},{5,5},{6,9},{7,13},{8,2},{9,6},{10,... | collective-permute-start | bytes 786440 | tf_op jit(solution)/shard_map/ppermute | solution.py:311
Sparse Core Ops, SparseCore 0:
  29.2 29.0 reduce-scatter.5
  60.7 25.7 reduce-scatter.3
  88.1 26.5 all-gather.2
  116.1 27.4 all-gather.4
  145.7 26.6 reduce-scatter.7
